TPU v7x, 32 devices: a whole 2x2x4 slice. The times are simulated.
32 devices in a mesh: seq: 4 (over x, core), fsdp: 8 (over z, y).
Axes of the slice: x: 2, y: 2, z: 4, core: 2. Of those that a mesh axis runs over, the one named last changes fastest.
Arguments:
- hidden_in: bfloat16 [8, 1024, 1536], P('fsdp', 'seq'), may hold values from -6 to 6
- positions: int32 [8, 1024], P('fsdp', 'seq'), may hold values from 0 to 5116, as said below
- attn_gain: bfloat16 [1536], P('fsdp'), may hold values from 0.25 to 1.75
- qkv_weight: bfloat16 [1536, 2048], P('fsdp'), may hold values from -0.15625 to 0.15625
- qkv_bias: bfloat16 [2048], P('fsdp'), may hold values from -3 to 3
- out_weight: bfloat16 [1536, 1536], P('fsdp'), may hold values from -1.75 to 1.75
- mlp_gain: bfloat16 [1536], P('fsdp'), may hold values from 0.25 to 1.75
- gate_weight: bfloat16 [8960, 1536], P('fsdp'), may hold values from -0.15625 to 0.15625
- up_weight: bfloat16 [8960, 1536], P('fsdp'), may hold values from -0.15625 to 0.15625
- down_weight: bfloat16 [8960, 1536], P('fsdp'), may hold values from -0.0625 to 0.0625
- cotangent: bfloat16 [8, 1024, 1536], P('fsdp', 'seq'), may hold values from -6 to 6
Outputs:
- hidden_out: bfloat16 [8, 1024, 1536], P('fsdp', 'seq')
- grad_in: float32 [8, 1024, 1536], P('fsdp', 'seq')
- grad_attn_gain: float32 [1536], P('fsdp')
- grad_qkv_weight: float32 [1536, 2048], P('fsdp')
- grad_qkv_bias: float32 [2048], P('fsdp')
- grad_out_weight: float32 [1536, 1536], P('fsdp')
- grad_mlp_gain: float32 [1536], P('fsdp')
- grad_gate_weight: float32 [8960, 1536], P('fsdp')
- grad_up_weight: float32 [8960, 1536], P('fsdp')
- grad_down_weight: float32 [8960, 1536], P('fsdp')
Inputs may be any that keep to these rules, and one draw needn't show every extreme that they name: Along each sequence the positions rise by 1 to 3 from one token to the next; the first lies below 2048.
All inputs are finite; a program needn't handle non-finite values.
Results may differ from a plain program's by a relative error of at most 0.019.
Values may be sent and summed in bfloat16 or wider, within the bound.
A program may use at most 320 MiB of HBM per device.

v0:
```python
import math

import jax
import jax.numpy as jnp
from jax import lax
from jax.sharding import PartitionSpec as P

HEADS = 12
KV_HEADS = 2
HEAD_DIM = 128


norm_eps = 1e-06
rope_base = 1000000.0


def rope_tables(position_row):
    half_dim = HEAD_DIM // 2
    frequency = jnp.exp(
        -(jnp.arange(half_dim, dtype=jnp.float32) * 2.0 / HEAD_DIM) * math.log(rope_base)
    )
    angles = position_row.astype(jnp.float32)[:, None] * frequency[None, :]
    angles = jnp.concatenate([angles, angles], axis=-1)
    return (jnp.cos(angles), jnp.sin(angles))


def rotate(values, cosine, sine):
    half_dim = values.shape[-1] // 2
    turned = jnp.concatenate([-values[..., half_dim:], values[..., :half_dim]], axis=-1)
    return values * cosine[:, None, :] + turned * sine[:, None, :]


def unrotate(grads_rot, cosine, sine):
    half_dim = grads_rot.shape[-1] // 2
    scaled = grads_rot * sine[:, None, :]
    return grads_rot * cosine[:, None, :] + jnp.concatenate(
        [scaled[..., half_dim:], -scaled[..., :half_dim]], axis=-1
    )


def norm_forward(values, gain):
    inverse = lax.rsqrt(jnp.mean(values * values, axis=-1, keepdims=True) + norm_eps)
    unit_rows = values * inverse
    return (unit_rows, inverse, (unit_rows * gain).astype(jnp.bfloat16))


def norm_backward(grad_normed, unit_rows, inverse, gain):
    grad_unit = grad_normed * gain
    grad_values = inverse * (
        grad_unit - unit_rows * jnp.mean(grad_unit * unit_rows, axis=-1, keepdims=True)
    )
    grad_gain = jnp.sum(grad_normed * unit_rows, axis=0)
    return (grad_values, grad_gain)


def masked_scores(queries, keys, block_start, block_rows):
    length = keys.shape[0]
    query_block = lax.dynamic_slice_in_dim(queries, block_start, block_rows, 0)
    scores = jnp.einsum(
        "bhd,ld->hbl", query_block, keys, preferred_element_type=jnp.float32
    ) * HEAD_DIM ** (-0.5)
    row_index = block_start + jnp.arange(block_rows)
    column_index = jnp.arange(length)
    allowed = column_index[None, :] <= row_index[:, None]
    return (query_block, jnp.where(allowed[None], scores, -1e30))


def attend_forward(queries, keys, values):
    length = keys.shape[0]
    block_rows = min(512, length)
    block_count = length // block_rows

    def one_block(block_start):
        query_block, scores = masked_scores(queries, keys, block_start, block_rows)
        row_max = jnp.max(scores, axis=-1, keepdims=True)
        exponent = jnp.exp(scores - row_max)
        row_total = jnp.sum(exponent, axis=-1, keepdims=True)
        probability = (exponent / row_total).astype(jnp.bfloat16)
        result = jnp.einsum("hbl,ld->bhd", probability, values, preferred_element_type=jnp.float32)
        return (result.astype(jnp.bfloat16), (row_max + jnp.log(row_total))[..., 0])

    results, log_totals = lax.map(one_block, jnp.arange(block_count) * block_rows)
    return (results.reshape(length, queries.shape[1], queries.shape[2]), log_totals)


def attend_backward(queries, keys, values, log_totals, grad_out):
    length = keys.shape[0]
    block_rows = min(512, length)
    block_count = length // block_rows
    score_scale = HEAD_DIM ** (-0.5)

    def one_block(running, inputs):
        grad_keys, grad_values = running
        block_start, log_block = inputs
        query_block, scores = masked_scores(queries, keys, block_start, block_rows)
        grad_block = lax.dynamic_slice_in_dim(grad_out, block_start, block_rows, 0)
        probability = jnp.exp(scores - log_block[..., None])
        grad_probs = jnp.einsum(
            "bhd,ld->hbl", grad_block, values, preferred_element_type=jnp.float32
        )
        row_delta = jnp.sum(probability * grad_probs, axis=-1, keepdims=True)
        grad_scores = (probability * (grad_probs - row_delta)).astype(jnp.bfloat16)
        grad_query = (
            jnp.einsum("hbl,ld->bhd", grad_scores, keys, preferred_element_type=jnp.float32)
            * score_scale
        )
        grad_keys = (
            grad_keys
            + jnp.einsum(
                "hbl,bhd->ld", grad_scores, query_block, preferred_element_type=jnp.float32
            )
            * score_scale
        )
        grad_values = grad_values + jnp.einsum(
            "hbl,bhd->ld",
            probability.astype(jnp.bfloat16),
            grad_block,
            preferred_element_type=jnp.float32,
        )
        return ((grad_keys, grad_values), grad_query)

    zero_rows = jnp.zeros((length, keys.shape[1]), jnp.float32)
    (grad_keys, grad_values), grad_query = lax.scan(
        one_block, (zero_rows, zero_rows), (jnp.arange(block_count) * block_rows, log_totals)
    )
    return (grad_query.reshape(queries.shape), grad_keys, grad_values)


def per_device(
    hidden_in,
    positions,
    attn_gain,
    qkv_weight,
    qkv_bias,
    out_weight,
    mlp_gain,
    gate_weight,
    up_weight,
    down_weight,
    cotangent,
):
    groups = lax.axis_size("seq")
    group_heads = HEADS // groups
    repeat = groups // KV_HEADS
    tokens = hidden_in.shape[1]
    width_query = HEADS * HEAD_DIM
    width_key = KV_HEADS * HEAD_DIM
    residual = hidden_in[0].astype(jnp.float32)
    cosine, sine = rope_tables(positions[0])
    gains_one, gains_two, qkv_full, bias_full, out_full = (
        lax.all_gather(attn_gain, "fsdp", axis=0, tiled=True),
        lax.all_gather(mlp_gain, "fsdp", axis=0, tiled=True),
        lax.all_gather(qkv_weight, "fsdp", axis=0, tiled=True),
        lax.all_gather(qkv_bias, "fsdp", axis=0, tiled=True),
        lax.all_gather(out_weight, "fsdp", axis=0, tiled=True),
    )
    gain_one = gains_one.astype(jnp.float32)
    gain_two = gains_two.astype(jnp.float32)
    unit_one, inverse_one, normed_one = norm_forward(residual, gain_one)
    qkv_mixed = jnp.dot(
        normed_one, qkv_full, preferred_element_type=jnp.float32
    ) + bias_full.astype(jnp.float32)
    query_part = qkv_mixed[:, :width_query].reshape(tokens, HEADS, HEAD_DIM)
    key_part = qkv_mixed[:, width_query : width_query + width_key].reshape(
        tokens, KV_HEADS, HEAD_DIM
    )
    value_part = qkv_mixed[:, width_query + width_key :].reshape(tokens, KV_HEADS, HEAD_DIM)
    queries = (
        rotate(query_part, cosine, sine)
        .astype(jnp.bfloat16)
        .reshape(tokens, groups, group_heads * HEAD_DIM)
    )
    keys_rep = jnp.repeat(rotate(key_part, cosine, sine).astype(jnp.bfloat16), repeat, axis=1)
    values_rep = jnp.repeat(value_part.astype(jnp.bfloat16), repeat, axis=1)
    head_queries, head_keys, head_values = (
        lax.all_to_all(queries, "seq", split_axis=1, concat_axis=0, tiled=True),
        lax.all_to_all(keys_rep, "seq", split_axis=1, concat_axis=0, tiled=True),
        lax.all_to_all(values_rep, "seq", split_axis=1, concat_axis=0, tiled=True),
    )
    head_queries = head_queries.reshape(-1, group_heads, HEAD_DIM)
    head_keys = head_keys.reshape(-1, HEAD_DIM)
    head_values = head_values.reshape(-1, HEAD_DIM)
    attended, log_totals = attend_forward(head_queries, head_keys, head_values)
    returned = lax.all_to_all(
        attended.reshape(-1, 1, group_heads * HEAD_DIM),
        "seq",
        split_axis=0,
        concat_axis=1,
        tiled=True,
    )
    attn_rows = returned.reshape(tokens, width_query)
    residual_two = residual + jnp.dot(attn_rows, out_full, preferred_element_type=jnp.float32)
    unit_two, inverse_two, normed_two = norm_forward(residual_two, gain_two)
    grad_output = cotangent[0].astype(jnp.float32)
    grad_mlp = grad_output.astype(jnp.bfloat16)
    all_rows = lax.all_gather(normed_two, "fsdp", axis=0, tiled=True)
    gate_pre = jnp.einsum("td,fd->tf", all_rows, gate_weight, preferred_element_type=jnp.float32)
    up_pre = jnp.einsum("td,fd->tf", all_rows, up_weight, preferred_element_type=jnp.float32)
    sigmoid_gate = jax.nn.sigmoid(gate_pre)
    activated = gate_pre * sigmoid_gate
    hidden = (activated * up_pre).astype(jnp.bfloat16)
    partial_out = jnp.dot(hidden, down_weight, preferred_element_type=jnp.float32)
    mlp_out = lax.psum_scatter(
        partial_out.astype(jnp.bfloat16), "fsdp", scatter_dimension=0, tiled=True
    ).astype(jnp.float32)
    all_grads = lax.all_gather(grad_mlp, "fsdp", axis=0, tiled=True)
    grad_hidden = jnp.einsum(
        "tm,fm->tf", all_grads, down_weight, preferred_element_type=jnp.float32
    )
    grad_gate = (
        grad_hidden * up_pre * sigmoid_gate * (1.0 + gate_pre * (1.0 - sigmoid_gate))
    ).astype(jnp.bfloat16)
    grad_up = (grad_hidden * activated).astype(jnp.bfloat16)
    partial_back = jnp.dot(grad_gate, gate_weight, preferred_element_type=jnp.float32) + jnp.dot(
        grad_up, up_weight, preferred_element_type=jnp.float32
    )
    grad_normed_two = lax.psum_scatter(partial_back, "fsdp", scatter_dimension=0, tiled=True)
    shard_gate = jnp.einsum("tf,td->fd", grad_gate, all_rows, preferred_element_type=jnp.float32)
    shard_up = jnp.einsum("tf,td->fd", grad_up, all_rows, preferred_element_type=jnp.float32)
    shard_down = jnp.einsum("tf,td->fd", hidden, all_grads, preferred_element_type=jnp.float32)
    hidden_out = (residual_two + mlp_out).astype(jnp.bfloat16)
    grad_norm_two, term_gain_two = norm_backward(grad_normed_two, unit_two, inverse_two, gain_two)
    grad_residual_two = grad_output + grad_norm_two
    grad_proj = grad_residual_two.astype(jnp.bfloat16)
    grad_attn_rows = jnp.einsum(
        "td,ed->te", grad_proj, out_full, preferred_element_type=jnp.float32
    ).astype(jnp.bfloat16)
    term_out = jnp.einsum("te,td->ed", attn_rows, grad_proj, preferred_element_type=jnp.float32)
    grad_heads = lax.all_to_all(
        grad_attn_rows.reshape(tokens, groups, group_heads * HEAD_DIM),
        "seq",
        split_axis=1,
        concat_axis=0,
        tiled=True,
    )
    grad_query, grad_keys, grad_values = attend_backward(
        head_queries,
        head_keys,
        head_values,
        log_totals,
        grad_heads.reshape(-1, group_heads, HEAD_DIM),
    )
    back_query, back_keys, back_values = (
        lax.all_to_all(
            grad_query.astype(jnp.bfloat16).reshape(-1, 1, group_heads * HEAD_DIM),
            "seq",
            split_axis=0,
            concat_axis=1,
            tiled=True,
        ),
        lax.all_to_all(
            grad_keys.astype(jnp.bfloat16)[:, None, :],
            "seq",
            split_axis=0,
            concat_axis=1,
            tiled=True,
        ),
        lax.all_to_all(
            grad_values.astype(jnp.bfloat16)[:, None, :],
            "seq",
            split_axis=0,
            concat_axis=1,
            tiled=True,
        ),
    )
    grad_query_rows = unrotate(
        back_query.reshape(tokens, HEADS, HEAD_DIM).astype(jnp.float32), cosine, sine
    )
    grad_key_rows = unrotate(
        jnp.sum(back_keys.astype(jnp.float32).reshape(tokens, KV_HEADS, repeat, HEAD_DIM), axis=2),
        cosine,
        sine,
    )
    grad_value_rows = jnp.sum(
        back_values.astype(jnp.float32).reshape(tokens, KV_HEADS, repeat, HEAD_DIM), axis=2
    )
    grad_mixed = jnp.concatenate(
        [
            grad_query_rows.reshape(tokens, width_query),
            grad_key_rows.reshape(tokens, width_key),
            grad_value_rows.reshape(tokens, width_key),
        ],
        axis=1,
    ).astype(jnp.bfloat16)
    term_qkv = jnp.einsum("td,tc->dc", normed_one, grad_mixed, preferred_element_type=jnp.float32)
    term_bias = jnp.sum(grad_mixed.astype(jnp.float32), axis=0)
    grad_normed_one = jnp.einsum(
        "tc,dc->td", grad_mixed, qkv_full, preferred_element_type=jnp.float32
    )
    grad_norm_one, term_gain_one = norm_backward(grad_normed_one, unit_one, inverse_one, gain_one)
    grad_rows = grad_residual_two + grad_norm_one
    shard_gain_one, shard_qkv, shard_bias, shard_out, shard_gain_two = (
        lax.psum_scatter(
            term_gain_one.astype(jnp.bfloat16), "fsdp", scatter_dimension=0, tiled=True
        ).astype(jnp.float32),
        lax.psum_scatter(
            term_qkv.astype(jnp.bfloat16), "fsdp", scatter_dimension=0, tiled=True
        ).astype(jnp.float32),
        lax.psum_scatter(
            term_bias.astype(jnp.bfloat16), "fsdp", scatter_dimension=0, tiled=True
        ).astype(jnp.float32),
        lax.psum_scatter(
            term_out.astype(jnp.bfloat16), "fsdp", scatter_dimension=0, tiled=True
        ).astype(jnp.float32),
        lax.psum_scatter(
            term_gain_two.astype(jnp.bfloat16), "fsdp", scatter_dimension=0, tiled=True
        ).astype(jnp.float32),
    )
    totals = (
        lax.psum(shard_gain_one.astype(jnp.bfloat16), "seq").astype(jnp.float32),
        lax.psum(shard_qkv.astype(jnp.bfloat16), "seq").astype(jnp.float32),
        lax.psum(shard_bias.astype(jnp.bfloat16), "seq").astype(jnp.float32),
        lax.psum(shard_out.astype(jnp.bfloat16), "seq").astype(jnp.float32),
        lax.psum(shard_gain_two.astype(jnp.bfloat16), "seq").astype(jnp.float32),
        lax.psum(shard_gate.astype(jnp.bfloat16), "seq").astype(jnp.float32),
        lax.psum(shard_up.astype(jnp.bfloat16), "seq").astype(jnp.float32),
        lax.psum(shard_down.astype(jnp.bfloat16), "seq").astype(jnp.float32),
    )
    return (
        hidden_out[None],
        grad_rows[None],
        totals[0],
        totals[1],
        totals[2],
        totals[3],
        totals[4],
        totals[5],
        totals[6],
        totals[7],
    )


def solution(mesh):
    placed = (
        P("fsdp", "seq", None),
        P("fsdp", "seq"),
        P("fsdp"),
        P("fsdp", None),
        P("fsdp"),
        P("fsdp", None),
        P("fsdp"),
        P("fsdp", None),
        P("fsdp", None),
        P("fsdp", None),
        P("fsdp", "seq", None),
    )
    return jax.shard_map(
        per_device,
        mesh=mesh,
        in_specs=placed,
        out_specs=(
            P("fsdp", "seq", None),
            P("fsdp", "seq", None),
            P("fsdp"),
            P("fsdp", None),
            P("fsdp"),
            P("fsdp", None),
            P("fsdp"),
            P("fsdp", None),
            P("fsdp", None),
            P("fsdp", None),
        ),
        check_vma=False,
    )
```

profile of v0, /device:TPU:2, one launch (start us, length us, event | category | flops | bytes accessed | tf_op | source)
XLA Modules:
  0.0 1277.5 jit_solution(13989524856095700904)
XLA Ops:
  12.4 22.4 %all-reduce.6 = (bf16[1536]{0:T(1024)(128)(2,1)S(1)}, bf16[1536]{0:T(1024)(128)(2,1)S(1)}) all-reduce(bf16[1536]{0:T(1024)(128)(2,1)S(1)} %dynamic-update-slice, bf16[1536]{0:T(1024)(128)(2,1)S(1)} %dynamic-update-slice.1), channel_id=1, replica_groups=mesh['seq'=4,'fsdp'=8] {'fsdp'}, use_global_device_ids=true, to_apply=%add | all-reduce | flops 3072 | bytes 12288
  36.9 16.5 %all-gather.1 = bf16[8,1,256]{2,1,0:T(2,128)(2,1)S(1)} all-gather(bf16[1,1,256]{2,1,0:T(2,128)(2,1)S(1)} %reshape.306), channel_id=1, replica_groups=mesh['seq'=4,'fsdp'=8] {'fsdp'}, dimensions={0}, use_global_device_ids=true | all-gather | bytes 4608 | tf_op jit(solution)/shard_map/all_gather | solution.py:154
  58.8 52.3 %all-gather.7.cloned.1.call-done = bf16[1536,2048]{1,0:T(8,128)(2,1)} async-done(((bf16[192,2048]{1,0:T(8,128)(2,1)}), bf16[1536,2048]{1,0:T(8,128)(2,1)}) %all-gather.7.cloned.1.call-update) | async-done | bytes 6291472 | tf_op jit(solution)/shard_map/all_gather | solution.py:153
  141.3 8.5 all-to-all-done
  151.4 5.8 all-to-all-start.2
  164.7 23.9 %while.27 = (s32[]{:T(128)}, bf16[2,512,3,128]{3,1,2,0:T(8,128)(2,1)}, f32[2,3,512]{2,1,0:T(4,128)S(1)}, s32[2]{0:T(128)S(1)}, bf16[1024,3,128]{2,0,1:T(8,128)(2...) while((s32[]{:T(128)}, ...), condition=%wide.region_4.5_spmd, body=%wide.region_1.4_spmd.sunk | while | flops 824900608 | bytes 22342304 | solution.py:82
  197.4 7.3 reduce.2
  211.0 10.0 all-to-all-done.3
  236.8 96.7 %all-gather.11.cloned.1.call-done = bf16[2048,1536]{1,0:T(8,128)(2,1)} async-done(((bf16[256,1536]{1,0:T(8,128)(2,1)}), bf16[2048,1536]{1,0:T(8,128)(2,1)}) %all-gather.11.cloned.1.call-update) | async-done | bytes 6291472 | tf_op jit(solution)/shard_map/all_gather | solution.py:196
  333.4 13.4 %fusion.80 = f32[2048,1120]{0,1:T(8,128)} fusion(bf16[2048,1536]{1,0:T(8,128)(2,1)} %all-gather.11.cloned.1.call-done, bf16[1120,1536]{1,0:T(8,128)(2,1)} %param.22), kind=kOutput, calls=%fused_computation.140 | convolution fusion | flops 7046430720 | bytes 18907136 | tf_op jit(solution)/shard_map/td,fd->tf/dot_general | solution.py:197
  346.8 9.6 fusion.81
  356.4 76.3 %all-gather.13.cloned.1.call-done = bf16[1,2048,1536]{2,1,0:T(8,128)(2,1)} async-done(((bf16[1,256,1536]{2,1,0:T(8,128)(2,1)}), bf16[1,2048,1536]{2,1,0:T(8,128)(2,1)}) %all-gather.13.cloned.1.call-update) | async-done | bytes 6291472 | tf_op jit(solution)/shard_map/all_gather | solution.py:206
  432.7 18.3 %multiply_convert_fusion = (bf16[2048,1120]{0,1:T(8,128)(2,1)}, bf16[2048,1120]{0,1:T(8,128)(2,1)}, bf16[2048,1120]{0,1:T(8,128)(2,1)}) fusion(f32[2048,1120]{0,1:T(8,128)} %fusion.80, f32[2048,1120]{0,1:T(8,128)} %fusion.81, bf16[1120,1536]{1,0:T(8,128)(2,1)S(1)} %copy-done, bf16[1,2048,1536]{2,1,0:T(8,128)(2,1)} %all-gather.13.cloned.1.call-done), kind=kOutput, calls=%fused_computation.56 | convolution fusion | flops 7080837120 | bytes 41844736 | tf_op jit(solution)/shard_map/tm,fm->tf/dot_general | solution.py:207
  451.0 13.0 %fusion.82 = f32[2048,1536]{1,0:T(8,128)} fusion(bf16[2048,1120]{0,1:T(8,128)(2,1)} %get-tuple-element.264, bf16[1120,1536]{1,0:T(8,128)(2,1)S(1)} %copy-done.31), kind=kOutput, calls=%fused_computation.142 | convolution fusion | flops 7046430720 | bytes 20611072 | tf_op jit(solution)/shard_map/dot_general | solution.py:214
  464.1 14.4 %convolution_add_fusion = f32[2048,1536]{1,0:T(8,128)} fusion(f32[2048,1536]{1,0:T(8,128)} %fusion.82, bf16[2048,1120]{0,1:T(8,128)(2,1)S(1)} %copy-done.34, bf16[1120,1536]{1,0:T(8,128)(2,1)S(1)} %copy-done.33), kind=kOutput, calls=%fused_computation.61 | convolution fusion | flops 7049576448 | bytes 33193984 | tf_op jit(solution)/shard_map/dot_general | solution.py:214
  478.5 12.4 convolution_convert_fusion
  491.0 193.2 %reduce-scatter.7.cloned.1.call-done = f32[256,1536]{1,0:T(8,128)} async-done(((f32[2048,1536]{1,0:T(8,128)}), f32[256,1536]{1,0:T(8,128)}) %reduce-scatter.7.cloned.1.call-update) | async-done | bytes 1572880 | tf_op jit(solution)/shard_map/reduce_scatter | solution.py:217
  686.7 118.6 %reduce-scatter.5.cloned.1.call-done = bf16[256,1536]{1,0:T(8,128)(2,1)} async-done(((bf16[2048,1536]{1,0:T(8,128)(2,1)}), bf16[256,1536]{1,0:T(8,128)(2,1)}) %reduce-scatter.5.cloned.1.call-update) | async-done | bytes 786448 | tf_op jit(solution)/shard_map/reduce_scatter | solution.py:203
  821.6 6.4 all-to-all-done.4
  829.2 46.6 %while.28 = (s32[]{:T(128)}, f32[1024,128]{1,0:T(8,128)}, f32[1024,128]{1,0:T(8,128)}, bf16[2,512,3,128]{3,1,2,0:T(8,128)(2,1)}, s32[2]{0:T(128)S(1)}, /*index=5...) while((s32[]{:T(128)}, f32[1024,128]{1,0:T(8,128)}, ...), condition=%wide.region_11.12_spmd.clone, body=%wide.region_9.11_spmd.clone.sunk | while | flops 2038234112 | bytes 90227544 | solution.py:123
  846.5 6.0 fusion.140
  869.7 6.1 fusion.140
  908.7 8.1 all-to-all-done.5
  927.0 12.5 convolution_convert_fusion.3
  939.4 12.1 convolution_convert_fusion.4
  951.6 8.8 convolution_convert_fusion.2
  960.4 84.0 %reduce-scatter.9.cloned.1.call-done = bf16[192,2048]{1,0:T(8,128)(2,1)} async-done(((bf16[1536,2048]{1,0:T(8,128)(2,1)}), bf16[192,2048]{1,0:T(8,128)(2,1)}) %reduce-scatter.9.cloned.1.call-update) | async-done | bytes 786448 | tf_op jit(solution)/shard_map/reduce_scatter | solution.py:296
  1046.1 6.1 fusion.60
  1052.2 35.3 %all-reduce.5 = (bf16[1536]{0:T(1024)(128)(2,1)S(1)}, bf16[2048]{0:T(1024)(128)(2,1)S(1)}, bf16[1536]{0:T(1024)(128)(2,1)S(1)}) all-reduce(bf16[1536]{0:T(1024)(128)(2,1)S(1)} %get-tuple-element.210, bf16[2048]{0:T(1024)(128)(2,1)S(1)} %fusion.75, bf16[1536]{0:T(1024)(128)(2,1)S(1)} %copy-done.29), channel_id=5, replica_groups=mesh['seq'=4,'fsdp'=8] {'fsdp'}, use_global_device_ids=true, to_apply=%region_16.17.clone | all-reduce | flops 5120 | bytes 20480
  1087.8 6.5 all-reduce.7
  1099.0 155.4 %all-reduce.11.cloned.1.call-done = (bf16[192,2048]{1,0:T(8,128)(2,1)}, bf16[192,1536]{1,0:T(8,128)(2,1)}, bf16[1120,1536]{1,0:T(8,128)(2,1)}, bf16[1120,1536]{1,0:T(8,128)(2,1)}, bf16[1120,1536]{1,0:T(8,128)(2,1)}) async-done(((bf16[192,2048]{1,0:T(8,128)(2,1)}, bf16[192,1536]{1,0:T(8,128)(2,1)}, bf16[1120,1536]{1,0:T(8,128)(2,1)}, bf16[1120,1536]{1,0:T(8,128)(2,1)}, bf16[1120,1536]{1,0:T(8,128)(2,1)}), ...) | async-done | bytes 11698192 | tf_op jit(solution)/shard_map/psum | solution.py:311
  1254.4 6.0 convert_element_type.265
  (252 shorter events, 211.1 us)
Async XLA Ops:
  7.2 425.5 %copy-start = (bf16[1120,1536]{1,0:T(8,128)(2,1)S(1)}, bf16[1120,1536]{1,0:T(8,128)(2,1)}, u32[]{:S(2)}) copy-start(bf16[1120,1536]{1,0:T(8,128)(2,1)} %param.24) | copy-start | bytes 10321924
  7.2 103.9 %all-gather.7.cloned.1.call-start = ((), (), s32[]{:S(2)}) async-start(), calls=%async_computation.12 | async-start | bytes 7077888 | tf_op jit(solution)/shard_map/all_gather | solution.py:153
  7.9 221.5 %all-gather.9.cloned.1.call-start = ((), (), s32[]{:S(2)}) async-start(), calls=%async_computation.13 | async-start | bytes 5308416 | tf_op jit(solution)/shard_map/all_gather | solution.py:155
  34.9 81.1 %copy-start.25 = (f32[1536]{0:T(1024)}, f32[1536]{0:T(1024)S(1)}, u32[]{:S(2)}) copy-start(f32[1536]{0:T(1024)S(1)} %convert_element_type.218) | copy-start | bytes 18436
  36.2 79.7 %copy-start.27 = (f32[256]{0:T(256)}, f32[256]{0:T(256)S(1)}, u32[]{:S(2)}) copy-start(f32[256]{0:T(256)S(1)} %add_rsqrt_fusion.1) | copy-start | bytes 3076
  124.8 9.0 all-to-all-start.1
  133.8 15.9 %all-to-all-start = ((bf16[256,4,384]{0,2,1:T(8,128)(2,1)}), bf16[256,4,384]{0,2,1:T(8,128)(2,1)}, u32[]{:S(2)}, u32[]{:S(2)}) async-start(bf16[256,4,384]{0,2,1:T(8,128)(2,1)} %fusion.63), calls=%async_computation | async-start | bytes 1572864 | tf_op jit(solution)/shard_map/all_to_all | solution.py:176
  151.4 13.3 %all-to-all-start.2 = ((bf16[256,4,128]{2,0,1:T(8,128)(2,1)}), bf16[256,4,128]{2,0,1:T(8,128)(2,1)}, u32[]{:S(2)}, u32[]{:S(2)}) async-start(bf16[256,4,128]{2,0,1:T(8,128)(2,1)} %bitcast.287), calls=%async_computation.2 | async-start | bytes 524288 | tf_op jit(solution)/shard_map/all_to_all | solution.py:178
  206.7 14.3 %all-to-all-start.3 = ((bf16[4,2,49152]{2,1,0:T(2,128)(2,1)}), bf16[4,2,49152]{2,1,0:T(2,128)(2,1)}, u32[]{:S(2)}, u32[]{:S(2)}) async-start(bf16[4,2,49152]{2,1,0:T(2,128)(2,1)} %reshape.324), calls=%async_computation.3 | async-start | bytes 1572864 | tf_op jit(solution)/shard_map/all_to_all | solution.py:184
  210.9 122.5 %all-gather.11.cloned.1.call-start = ((), (), s32[]{:S(2)}) async-start(), calls=%async_computation.14 | async-start | bytes 7077888 | tf_op jit(solution)/shard_map/all_gather | solution.py:196
  235.9 196.8 %all-gather.13.cloned.1.call-start = ((), (), s32[]{:S(2)}) async-start(), calls=%async_computation.19 | async-start | bytes 7077888 | tf_op jit(solution)/shard_map/all_gather | solution.py:206
  236.5 447.7 %reduce-scatter.7.cloned.1.call-start = ((), (), s32[]{:S(2)}) async-start(), calls=%async_computation.16 | async-start | bytes 14155776 | tf_op jit(solution)/shard_map/reduce_scatter | solution.py:217
  333.4 13.4 %copy-start.30 = (bf16[2048,1536]{1,0:T(8,128)(2,1)S(1)}, bf16[2048,1536]{1,0:T(8,128)(2,1)}, u32[]{:S(2)}) copy-start(bf16[2048,1536]{1,0:T(8,128)(2,1)} %all-gather.11.cloned.1.call-done) | copy-start | bytes 18874372
  333.4 13.4 %copy-start.32 = (bf16[1120,1536]{1,0:T(8,128)(2,1)S(1)}, bf16[1120,1536]{1,0:T(8,128)(2,1)}, u32[]{:S(2)}) copy-start(bf16[1120,1536]{1,0:T(8,128)(2,1)} %param.23) | copy-start | bytes 10321924
  432.7 18.3 %copy-start.31 = (bf16[1120,1536]{1,0:T(8,128)(2,1)S(1)}, bf16[1120,1536]{1,0:T(8,128)(2,1)}, u32[]{:S(2)}) copy-start(bf16[1120,1536]{1,0:T(8,128)(2,1)} %param.22) | copy-start | bytes 10321924
  451.0 13.0 %copy-start.33 = (bf16[1120,1536]{1,0:T(8,128)(2,1)S(1)}, bf16[1120,1536]{1,0:T(8,128)(2,1)}, u32[]{:S(2)}) copy-start(bf16[1120,1536]{1,0:T(8,128)(2,1)} %param.23) | copy-start | bytes 10321924
  451.0 13.0 %copy-start.34 = (bf16[2048,1120]{0,1:T(8,128)(2,1)S(1)}, bf16[2048,1120]{0,1:T(8,128)(2,1)}, u32[]{:S(2)}) copy-start(bf16[2048,1120]{0,1:T(8,128)(2,1)} %get-tuple-element.263) | copy-start | bytes 13762564
  478.5 326.8 %reduce-scatter.5.cloned.1.call-start = ((), (), s32[]{:S(2)}) async-start(), calls=%async_computation.15 | async-start | bytes 7077888 | tf_op jit(solution)/shard_map/reduce_scatter | solution.py:203
  491.0 193.2 %copy-start.6 = (f32[256,1536]{1,0:T(8,128)S(1)}, f32[256,1536]{1,0:T(8,128)}, u32[]{:S(2)}) copy-start(f32[256,1536]{1,0:T(8,128)} %copy-done.5) | copy-start | bytes 4718596
  808.5 9.5 copy-start.10
  814.0 14.0 %all-to-all-start.4 = ((bf16[256,4,384]{0,2,1:T(8,128)(2,1)}), bf16[256,4,384]{0,2,1:T(8,128)(2,1)S(1)}, u32[]{:S(2)}, u32[]{:S(2)}) async-start(bf16[256,4,384]{0,2,1:T(8,128)(2,1)} %bitcast.275), calls=%async_computation.6 | async-start | bytes 1572864 | tf_op jit(solution)/shard_map/all_to_all | solution.py:229
  818.0 142.4 %reduce-scatter.11.cloned.1.call-start = ((), (), s32[]{:S(2)}) async-start(), calls=%async_computation.18 | async-start | bytes 5308416 | tf_op jit(solution)/shard_map/reduce_scatter | solution.py:302
  878.7 9.4 all-to-all-start.6
  888.0 15.2 %all-to-all-start.7 = ((bf16[4,2,16384]{2,1,0:T(2,128)(2,1)}), bf16[4,2,16384]{2,1,0:T(2,128)(2,1)S(1)}, u32[]{:S(2)}, u32[]{:S(2)}) async-start(bf16[4,2,16384]{2,1,0:T(2,128)(2,1)} %reshape.326), calls=%async_computation.9 | async-start | bytes 524288 | tf_op jit(solution)/shard_map/all_to_all | solution.py:258
  903.3 13.5 %all-to-all-start.5 = ((bf16[4,2,49152]{2,1,0:T(2,128)(2,1)}), bf16[4,2,49152]{2,1,0:T(2,128)(2,1)S(1)}, u32[]{:S(2)}, u32[]{:S(2)}) async-start(bf16[4,2,49152]{2,1,0:T(2,128)(2,1)} %reshape.330), calls=%async_computation.7 | async-start | bytes 1572864 | tf_op jit(solution)/shard_map/all_to_all | solution.py:244
  906.8 137.7 %reduce-scatter.9.cloned.1.call-start = ((), (), s32[]{:S(2)}) async-start(), calls=%async_computation.17 | async-start | bytes 7077888 | tf_op jit(solution)/shard_map/reduce_scatter | solution.py:296
  926.9 327.4 %all-reduce.11.cloned.1.call-start = ((), (), s32[]{:S(2)}) async-start(), calls=%async_computation.20 | async-start | bytes 23396352 | tf_op jit(solution)/shard_map/psum | solution.py:311
  927.0 24.6 %slice-start = ((s8[6291456]{0:T(1024)(128)(4,1)}), s8[4194304]{0:T(1024)(128)(4,1)S(1)}, s32[]{:S(2)}) async-start(s8[6291456]{0:T(1024)(128)(4,1)} %bitcast.290), calls=%async_computation.21 | async-start | bytes 8388608
  927.0 24.6 %slice-start.2 = ((s8[4587520]{0:T(1024)(128)(4,1)}), s8[4194304]{0:T(1024)(128)(4,1)S(1)}, s32[]{:S(2)}) async-start(s8[4587520]{0:T(1024)(128)(4,1)} %bitcast.292), calls=%async_computation.23 | async-start | bytes 8388608
  939.4 12.1 slice-start.1
  939.4 12.1 slice-start.3
  1046.1 49.9 %copy-start.11 = (f32[256,1536]{1,0:T(8,128)S(1)}, f32[256,1536]{1,0:T(8,128)}, u32[]{:S(2)}) copy-start(f32[256,1536]{1,0:T(8,128)} %copy-done.10) | copy-start | bytes 4718596
  (29 other events, 114.7 us)
Sparse Core Ops, SparseCore 0:
  10.2 100.7 all-gather.6
  113.2 78.0 all-gather.8
  236.1 97.3 all-gather.10
  335.5 97.2 all-gather.12
  478.6 205.5 reduce-scatter.6
  688.2 116.9 reduce-scatter.4
  823.1 94.3 reduce-scatter.10
  927.0 117.3 reduce-scatter.8
  1048.0 206.2 all-reduce.10
where the time goes:
time: 1290 us; the launch traced here: 1280 us
  waiting for transfers between devices  815 us (63%)
  matrix products  191 us (15%)
  blocking collectives  80.7 us (6%)
  other arithmetic  66.4 us (5%)
  local copies, waits for them, and re-layouts  61.1 us (5%)
  starting transfers between devices  38.7 us (3%)
  between operations  16.9 us (1%)
    reduce_scatter x1, waiting for transfers between devices, per_device(): lax.psum_scatter(partial_back, 'fsdp', scatter_dimension=0, tiled=True)  193 us
    psum x1, waiting for transfers between devices, per_device(): lax.psum(shard_qkv.astype(jnp.bfloat16), 'seq').astype(jnp.float32)  155 us
    reduce_scatter x1, waiting for transfers between devices, per_device(): lax.psum_scatter(partial_out.astype(jnp.bfloat16), 'fsdp', scatter_dimens...  119 us
    all_gather x1, waiting for transfers between devices, per_device(): all_rows = lax.all_gather(normed_two, 'fsdp', axis=0, tiled=True)  96.7 us
    reduce_scatter x1, waiting for transfers between devices, per_device(): lax.psum_scatter(term_qkv.astype(jnp.bfloat16), 'fsdp', scatter_dimension...  84 us
    all_gather x1, waiting for transfers between devices, per_device(): all_grads = lax.all_gather(grad_mlp, 'fsdp', axis=0, tiled=True)  76.3 us
    unnamed x2, blocking collectives  57.7 us
    all_gather x1, waiting for transfers between devices, per_device(): lax.all_gather(qkv_weight, 'fsdp', axis=0, tiled=True)  52.3 us
  transfers between devices with their start and end apart: 17, of which 13 were waited for; matrix products, arithmetic and copies ran while one was open for 19% of the time, Pallas kernels for 0%

commit v1 on v0

--- a/solution.py
+++ b/solution.py
@@ -1,8 +1,11 @@
+import functools
 import math
 
 import jax
 import jax.numpy as jnp
 from jax import lax
+from jax.experimental import pallas as pl
+from jax.experimental.pallas import tpu as pltpu
 from jax.sharding import PartitionSpec as P
 
 HEADS = 12
@@ -126,6 +129,332 @@
     return (grad_query.reshape(queries.shape), grad_keys, grad_values)
 
 
+MESH = pl.DeviceIdType.MESH
+VMEM_BYTES = 67_000_000
+NN = (((1,), (0,)), ((), ()))
+NT = (((1,), (1,)), ((), ()))
+TN = (((0,), (0,)), ((), ()))
+
+
+def matmul(left, right, dims):
+    return lax.dot_general(left, right, dims, preferred_element_type=jnp.float32)
+
+
+def ring_place(index, size):
+    side = index % 2
+    return (index // 2) * (1 - side) + (size - 1 - index // 2) * side
+
+
+def ring_member(place, size):
+    side = place // (size // 2)
+    return 2 * (place * (1 - side) + (size - 1 - place) * side) + side
+
+
+def for_blocks(width, block, body):
+    @pl.loop(0, width // block)
+    def _(at):
+        body(pl.ds(pl.multiple_of(at * block, block), block))
+
+    if width % block:
+        body(pl.ds(width - width % block, width % block))
+
+
+def mlp_kernel(
+    size,
+    rows_ref,
+    cot_ref,
+    gate_ref,
+    up_ref,
+    down_ref,
+    parts_ref,
+    back_ref,
+    grad_gate_ref,
+    grad_up_ref,
+    grad_down_ref,
+    rows_all,
+    cots_all,
+    weights,
+    grads,
+    hid,
+    dgate,
+    dup,
+    partial,
+    sums_in,
+    sums_out,
+    parts_out,
+    load_sems,
+    send_sems,
+    recv_sems,
+    sum_send_sems,
+    sum_recv_sems,
+    part_sems,
+):
+    tokens, width = rows_ref.shape
+    units = gate_ref.shape[0]
+    half = tokens // 2
+    me = lax.axis_index("fsdp")
+    place = ring_place(me, size)
+    right = ring_member((place + 1) % size, size)
+    left = ring_member((place + size - 1) % size, size)
+    sides = ((right, pl.ds(0, half)), (left, pl.ds(half, half)))
+
+    weight_loads = [
+        pltpu.make_async_copy(ref, weights.at[at], load_sems.at[at])
+        for at, ref in enumerate((gate_ref, up_ref, down_ref))
+    ]
+    own_loads = [
+        pltpu.make_async_copy(rows_ref, rows_all.at[0], load_sems.at[3]),
+        pltpu.make_async_copy(cot_ref, cots_all.at[0], load_sems.at[4]),
+    ]
+    for load in own_loads + weight_loads:
+        load.start()
+    barrier = pltpu.get_barrier_semaphore()
+    for target, _ in sides:
+        pl.semaphore_signal(barrier, inc=1, device_id={"fsdp": target}, device_id_type=MESH)
+
+    @pl.loop(0, units // 16)
+    def _(at):
+        zeros = jnp.zeros((3, 16, width), jnp.float32)
+        grads[:, pl.ds(pl.multiple_of(at * 16, 16), 16), :] = zeros
+
+    pl.semaphore_wait(barrier, 2)
+    for load in own_loads:
+        load.wait()
+
+    def row_copy(step, side, which):
+        held = (rows_all, cots_all)[which]
+        target, span = sides[side]
+        return pltpu.make_async_remote_copy(
+            src_ref=held.at[step, span],
+            dst_ref=held.at[step + 1, span],
+            send_sem=send_sems.at[side, which, step],
+            recv_sem=recv_sems.at[side, which, step + 1],
+            device_id={"fsdp": target},
+            device_id_type=MESH,
+        )
+
+    def sum_copy(step, side):
+        target, span = sides[side]
+        return pltpu.make_async_remote_copy(
+            src_ref=sums_out.at[step % 2, span],
+            dst_ref=sums_in.at[step, span],
+            send_sem=sum_send_sems.at[side, step],
+            recv_sem=sum_recv_sems.at[side, step],
+            device_id={"fsdp": target},
+            device_id_type=MESH,
+        )
+
+    def part_copy(step, side):
+        _, span = sides[side]
+        away = step if side == 1 else size - step
+        owner = ring_member((place + away) % size, size)
+        return pltpu.make_async_copy(
+            parts_out.at[step % 2, span],
+            parts_ref.at[pl.ds(pl.multiple_of(owner * tokens + side * half, half), half)],
+            part_sems.at[side, step],
+        )
+
+    def elementwise(step, span):
+        gate = matmul(rows_all[step], weights[0, span, :], NT)
+        up = matmul(rows_all[step], weights[1, span, :], NT)
+        grad_hidden = matmul(cots_all[step], weights[2, span, :], NT)
+        sigmoid = jax.nn.sigmoid(gate)
+        activated = gate * sigmoid
+        hid[:, span] = (activated * up).astype(jnp.bfloat16)
+        dgate[:, span] = (
+            grad_hidden * up * sigmoid * (1.0 + gate * (1.0 - sigmoid))
+        ).astype(jnp.bfloat16)
+        dup[:, span] = (grad_hidden * activated).astype(jnp.bfloat16)
+
+    for load in weight_loads:
+        load.wait()
+
+    @pl.loop(0, size)
+    def _(step):
+        slot = step % 2
+
+        @pl.when(step >= 1)
+        def _():
+            for side in range(2):
+                for which in range(2):
+                    row_copy(step - 1, side, which).wait_recv()
+
+        @pl.when(step < size - 1)
+        def _():
+            for side in range(2):
+                for which in range(2):
+                    row_copy(step, side, which).start()
+
+        for_blocks(units, 256, functools.partial(elementwise, step))
+
+        def back_part(span):
+            partial[:, span] = matmul(dgate[...], weights[0, :, span], NN) + matmul(
+                dup[...], weights[1, :, span], NN
+            )
+
+        for_blocks(width, 256, back_part)
+
+        @pl.when(step == 0)
+        def _():
+            back_ref[...] = partial[...]
+
+        @pl.when(step >= 3)
+        def _():
+            for side in range(2):
+                sum_copy(step - 2, side).wait_send()
+
+        @pl.when(step == 1)
+        def _():
+            sums_out[slot] = partial[...].astype(jnp.bfloat16)
+
+        @pl.when(step >= 2)
+        def _():
+            for side in range(2):
+                sum_copy(step - 1, side).wait_recv()
+            sums_out[slot] = (partial[...] + sums_in[step - 1].astype(jnp.float32)).astype(
+                jnp.bfloat16
+            )
+
+        @pl.when(step >= 1)
+        def _():
+            for side in range(2):
+                sum_copy(step, side).start()
+
+        @pl.when(step >= 2)
+        def _():
+            for side in range(2):
+                part_copy(step - 2, side).wait()
+
+        def out_part(span):
+            parts_out[slot, :, span] = matmul(hid[...], weights[2, :, span], NN).astype(
+                jnp.bfloat16
+            )
+
+        for_blocks(width, 256, out_part)
+        for side in range(2):
+            part_copy(step, side).start()
+
+        def weight_part(span):
+            rows, cots = rows_all[step, :, span], cots_all[step, :, span]
+            grads[0, :, span] += matmul(dgate[...], rows, TN)
+            grads[1, :, span] += matmul(dup[...], rows, TN)
+            grads[2, :, span] += matmul(hid[...], cots, TN)
+
+        for_blocks(width, 256, weight_part)
+
+    stores = []
+    for at, ref in enumerate((grad_gate_ref, grad_up_ref, grad_down_ref)):
+
+        @pl.loop(0, units // 16)
+        def _(block):
+            span = pl.ds(pl.multiple_of(block * 16, 16), 16)
+            weights[at, span, :] = grads[at, span, :].astype(jnp.bfloat16)
+
+        stores.append(pltpu.make_async_copy(weights.at[at], ref, load_sems.at[at]))
+        stores[-1].start()
+    for side in range(2):
+        sum_copy(size - 1, side).wait_recv()
+    back_ref[...] += sums_in[size - 1].astype(jnp.float32)
+    for side in range(2):
+        sum_copy(size - 2, side).wait_send()
+        sum_copy(size - 1, side).wait_send()
+        part_copy(size - 2, side).wait()
+        part_copy(size - 1, side).wait()
+
+        @pl.loop(0, size - 1)
+        def _(step):
+            for which in range(2):
+                row_copy(step, side, which).wait_send()
+
+    for store in stores:
+        store.wait()
+
+
+def mlp_scratch(size, tokens, width, units):
+    bf16, f32 = jnp.bfloat16, jnp.float32
+    dma = pltpu.SemaphoreType.DMA
+    return [
+        pltpu.VMEM((size, tokens, width), bf16),
+        pltpu.VMEM((size, tokens, width), bf16),
+        pltpu.VMEM((3, units, width), bf16),
+        pltpu.VMEM((3, units, width), f32),
+        pltpu.VMEM((tokens, units), bf16),
+        pltpu.VMEM((tokens, units), bf16),
+        pltpu.VMEM((tokens, units), bf16),
+        pltpu.VMEM((tokens, width), f32),
+        pltpu.VMEM((size, tokens, width), bf16),
+        pltpu.VMEM((2, tokens, width), bf16),
+        pltpu.VMEM((2, tokens, width), bf16),
+        dma((5,)),
+        dma((2, 2, size)),
+        dma((2, 2, size)),
+        dma((2, size)),
+        dma((2, size)),
+        dma((2, size)),
+    ]
+
+
+def mlp_fits(size, tokens, width, units):
+    if size % 2 or tokens % 32 or units % 16 or width % 256:
+        return False
+    held = 3 * size + 4
+    return 2 * tokens * width * (held + 4) + units * (18 * width + 6 * tokens) < 60_000_000
+
+
+def mlp_ring(rows, cots, gate_weight, up_weight, down_weight):
+    size = lax.axis_size("fsdp")
+    tokens, width = rows.shape
+    units = gate_weight.shape[0]
+    anywhere = pl.BlockSpec(memory_space=pl.ANY)
+    bf16 = jnp.bfloat16
+    return pl.pallas_call(
+        functools.partial(mlp_kernel, size),
+        out_shape=(
+            jax.ShapeDtypeStruct((size * tokens, width), bf16),
+            jax.ShapeDtypeStruct((tokens, width), jnp.float32),
+            jax.ShapeDtypeStruct((units, width), bf16),
+            jax.ShapeDtypeStruct((units, width), bf16),
+            jax.ShapeDtypeStruct((units, width), bf16),
+        ),
+        in_specs=[anywhere] * 5,
+        out_specs=(anywhere, pl.BlockSpec(memory_space=pltpu.VMEM), anywhere, anywhere, anywhere),
+        scratch_shapes=mlp_scratch(size, tokens, width, units),
+        compiler_params=pltpu.CompilerParams(
+            collective_id=0, has_side_effects=True, vmem_limit_bytes=VMEM_BYTES
+        ),
+        name="mlp_ring",
+    )(rows, cots, gate_weight, up_weight, down_weight)
+
+
+def mlp_gathered(rows, cots, gate_weight, up_weight, down_weight):
+    all_rows = lax.all_gather(rows, "fsdp", axis=0, tiled=True)
+    gate_pre = jnp.einsum("td,fd->tf", all_rows, gate_weight, preferred_element_type=jnp.float32)
+    up_pre = jnp.einsum("td,fd->tf", all_rows, up_weight, preferred_element_type=jnp.float32)
+    sigmoid_gate = jax.nn.sigmoid(gate_pre)
+    activated = gate_pre * sigmoid_gate
+    hidden = (activated * up_pre).astype(jnp.bfloat16)
+    partial_out = jnp.dot(hidden, down_weight, preferred_element_type=jnp.float32)
+    all_grads = lax.all_gather(cots, "fsdp", axis=0, tiled=True)
+    grad_hidden = jnp.einsum(
+        "tm,fm->tf", all_grads, down_weight, preferred_element_type=jnp.float32
+    )
+    grad_gate = (
+        grad_hidden * up_pre * sigmoid_gate * (1.0 + gate_pre * (1.0 - sigmoid_gate))
+    ).astype(jnp.bfloat16)
+    grad_up = (grad_hidden * activated).astype(jnp.bfloat16)
+    partial_back = jnp.dot(grad_gate, gate_weight, preferred_element_type=jnp.float32) + jnp.dot(
+        grad_up, up_weight, preferred_element_type=jnp.float32
+    )
+    grad_rows = lax.psum_scatter(partial_back, "fsdp", scatter_dimension=0, tiled=True)
+    return (
+        partial_out.astype(jnp.bfloat16),
+        grad_rows,
+        jnp.einsum("tf,td->fd", grad_gate, all_rows, preferred_element_type=jnp.float32),
+        jnp.einsum("tf,td->fd", grad_up, all_rows, preferred_element_type=jnp.float32),
+        jnp.einsum("tf,td->fd", hidden, all_grads, preferred_element_type=jnp.float32),
+    )
+
+
 def per_device(
     hidden_in,
     positions,
@@ -193,31 +522,14 @@
     unit_two, inverse_two, normed_two = norm_forward(residual_two, gain_two)
     grad_output = cotangent[0].astype(jnp.float32)
     grad_mlp = grad_output.astype(jnp.bfloat16)
-    all_rows = lax.all_gather(normed_two, "fsdp", axis=0, tiled=True)
-    gate_pre = jnp.einsum("td,fd->tf", all_rows, gate_weight, preferred_element_type=jnp.float32)
-    up_pre = jnp.einsum("td,fd->tf", all_rows, up_weight, preferred_element_type=jnp.float32)
-    sigmoid_gate = jax.nn.sigmoid(gate_pre)
-    activated = gate_pre * sigmoid_gate
-    hidden = (activated * up_pre).astype(jnp.bfloat16)
-    partial_out = jnp.dot(hidden, down_weight, preferred_element_type=jnp.float32)
-    mlp_out = lax.psum_scatter(
-        partial_out.astype(jnp.bfloat16), "fsdp", scatter_dimension=0, tiled=True
-    ).astype(jnp.float32)
-    all_grads = lax.all_gather(grad_mlp, "fsdp", axis=0, tiled=True)
-    grad_hidden = jnp.einsum(
-        "tm,fm->tf", all_grads, down_weight, preferred_element_type=jnp.float32
-    )
-    grad_gate = (
-        grad_hidden * up_pre * sigmoid_gate * (1.0 + gate_pre * (1.0 - sigmoid_gate))
-    ).astype(jnp.bfloat16)
-    grad_up = (grad_hidden * activated).astype(jnp.bfloat16)
-    partial_back = jnp.dot(grad_gate, gate_weight, preferred_element_type=jnp.float32) + jnp.dot(
-        grad_up, up_weight, preferred_element_type=jnp.float32
-    )
-    grad_normed_two = lax.psum_scatter(partial_back, "fsdp", scatter_dimension=0, tiled=True)
-    shard_gate = jnp.einsum("tf,td->fd", grad_gate, all_rows, preferred_element_type=jnp.float32)
-    shard_up = jnp.einsum("tf,td->fd", grad_up, all_rows, preferred_element_type=jnp.float32)
-    shard_down = jnp.einsum("tf,td->fd", hidden, all_grads, preferred_element_type=jnp.float32)
+    fits = mlp_fits(lax.axis_size("fsdp"), tokens, normed_two.shape[1], gate_weight.shape[0])
+    mlp = mlp_ring if fits else mlp_gathered
+    partial_out, grad_normed_two, shard_gate, shard_up, shard_down = mlp(
+        normed_two, grad_mlp, gate_weight, up_weight, down_weight
+    )
+    mlp_out = lax.psum_scatter(partial_out, "fsdp", scatter_dimension=0, tiled=True).astype(
+        jnp.float32
+    )
     hidden_out = (residual_two + mlp_out).astype(jnp.bfloat16)
     grad_norm_two, term_gain_two = norm_backward(grad_normed_two, unit_two, inverse_two, gain_two)
     grad_residual_two = grad_output + grad_norm_two

time: 1290 us -> 1000 us (0.78)
  waiting for transfers between devices: 815 us -> 484 us
  Pallas kernels: 0 us -> 189 us
  matrix products: 191 us -> 66.8 us
  local copies, waits for them, and re-layouts: 61.1 us -> 47.8 us
    reduce_scatter x2 -> x1, waiting for transfers between devices: 312 us -> 115 us  [per_device(): lax.psum_scatter(partial_out, 'fsdp', scatter_dimension=0, tiled=True)]
    pallas_call x0 -> x1, Pallas kernels: none -> 189 us  [mlp_ring(): pl.pallas_call(functools.partial(mlp_kernel, size), out_shape=(jax.ShapeD...]
    all_gather x2 -> x0, waiting for transfers between devices: 173 us -> none  [the longest x1 96.7 us: per_device(): all_rows = lax.all_gather(normed_two, 'fsdp', axis=0, tiled=True)]
    dot_general x9 -> x0, matrix products: 115 us -> none  [the longest x1 18.3 us: per_device(): jnp.einsum('tm,fm->tf', all_grads, down_weight, preferred_element_type=jn...]
    reduce_scatter x1, waiting for transfers between devices: 84 us -> 117 us  [per_device(): lax.psum_scatter(term_qkv.astype(jnp.bfloat16), 'fsdp', scatter_dimension...]
  transfers between devices with their start and end apart: 17 -> 14, of which waited for: 13 -> 11; matrix products, arithmetic and copies ran while one was open for 19% -> 14% of each run, Pallas kernels for 0% -> 0%
where the time goes in v1:
time: 1000 us; the launch traced here: 992 us
  waiting for transfers between devices  484 us (48%)
  Pallas kernels  189 us (19%)
  blocking collectives  80.8 us (8%)
  matrix products  66.8 us (7%)
  other arithmetic  59.8 us (6%)
  local copies, waits for them, and re-layouts  47.8 us (5%)
  starting transfers between devices  39.3 us (4%)
  between operations  17.1 us (2%)
    pallas_call x1, Pallas kernels, mlp_ring(): pl.pallas_call(functools.partial(mlp_kernel, size), out_shape=(jax.ShapeD...  189 us
    psum x1, waiting for transfers between devices, per_device(): lax.psum(shard_qkv.astype(jnp.bfloat16), 'seq').astype(jnp.float32)  155 us
    reduce_scatter x1, waiting for transfers between devices, per_device(): lax.psum_scatter(term_qkv.astype(jnp.bfloat16), 'fsdp', scatter_dimension...  117 us
    reduce_scatter x1, waiting for transfers between devices, per_device(): lax.psum_scatter(partial_out, 'fsdp', scatter_dimension=0, tiled=True)  115 us
    unnamed x2, blocking collectives  57.7 us
    all_gather x1, waiting for transfers between devices, per_device(): lax.all_gather(qkv_weight, 'fsdp', axis=0, tiled=True)  56.7 us
  transfers between devices with their start and end apart: 14, of which 11 were waited for; matrix products, arithmetic and copies ran while one was open for 14% of the time, Pallas kernels for 0%

profile of v1, /device:TPU:2, one launch (start us, length us, event | category | flops | bytes accessed | tf_op | source)
XLA Modules:
  0.0 992.3 jit_solution(5197766374794520501)
XLA Ops:
  12.4 22.4 %all-reduce.6 = (bf16[1536]{0:T(1024)(128)(2,1)S(1)}, bf16[1536]{0:T(1024)(128)(2,1)S(1)}) all-reduce(bf16[1536]{0:T(1024)(128)(2,1)S(1)} %dynamic-update-slice, bf16[1536]{0:T(1024)(128)(2,1)S(1)} %dynamic-update-slice.1), channel_id=1, replica_groups=mesh['seq'=4,'fsdp'=8] {'fsdp'}, use_global_device_ids=true, to_apply=%add | all-reduce | flops 3072 | bytes 12288
  36.3 16.5 %all-gather = bf16[8,1,256]{2,1,0:T(2,128)(2,1)S(1)} all-gather(bf16[1,1,256]{2,1,0:T(2,128)(2,1)S(1)} %reshape.304), channel_id=1, replica_groups=mesh['seq'=4,'fsdp'=8] {'fsdp'}, dimensions={0}, use_global_device_ids=true | all-gather | bytes 4608 | tf_op jit(solution)/shard_map/all_gather | solution.py:483
  54.4 56.7 %all-gather.4.cloned.1.call-done = bf16[1536,2048]{1,0:T(8,128)(2,1)} async-done(((bf16[192,2048]{1,0:T(8,128)(2,1)}), bf16[1536,2048]{1,0:T(8,128)(2,1)}) %all-gather.4.cloned.1.call-update) | async-done | bytes 6291472 | tf_op jit(solution)/shard_map/all_gather | solution.py:482
  111.1 4.6 convolution_add_fusion.1
  123.3 4.0 all-to-all-start.1
  131.7 5.1 all-to-all-start
  137.8 9.0 all-to-all-done
  147.5 5.3 all-to-all-start.2
  157.2 20.4 %while.27 = (s32[]{:T(128)}, bf16[2,512,3,128]{3,1,2,0:T(8,128)(2,1)}, f32[2,3,512]{2,1,0:T(4,128)S(1)}, s32[2]{0:T(128)S(1)}, bf16[1024,3,128]{2,0,1:T(8,128)(2...) while((s32[]{:T(128)}, ...), condition=%wide.region_4.5_spmd, body=%wide.region_1.4_spmd.sunk | while | flops 824900608 | bytes 28637404 | solution.py:85
  183.7 6.4 reduce.2
  191.1 5.1 all-to-all-start.3
  196.8 9.4 all-to-all-done.3
  209.4 4.1 multiply_reduce_fusion.2
  215.7 189.2 %mlp_ring.1 = (bf16[2048,1536]{1,0:T(8,128)(2,1)}, f32[256,1536]{1,0:T(8,128)}, bf16[1120,1536]{1,0:T(8,128)(2,1)}, bf16[1120,1536]{1,0:T(8,128)(2,1)}, bf16[1120,1536]{1,0:T(8,128)(2,1)}) custom-call(bf16[256,1536]{1,0:T(8,128)(2,1)} %multiply_convert_fusion.rows_ref, bf16[256,1536]{1,0:T(8,128)(2,1)} %bitcast.252, bf16[1120,1536]{1,0:T(8,128)(2,1)} %gate_ref.1, ...), custom_call_target="tpu_custom_call" | custom-call | tf_op jit(solution)/shard_map/mlp_ring/pallas_call | solution.py:410
  407.3 114.8 %reduce-scatter.4.cloned.1.call-done = bf16[256,1536]{1,0:T(8,128)(2,1)} async-done(((bf16[2048,1536]{1,0:T(8,128)(2,1)}), bf16[256,1536]{1,0:T(8,128)(2,1)}) %reduce-scatter.4.cloned.1.call-update) | async-done | bytes 786448 | tf_op jit(solution)/shard_map/reduce_scatter | solution.py:530
  525.3 4.3 convolution_convert_fusion.2
  530.8 4.7 all-to-all-start.4
  539.4 6.2 all-to-all-done.4
  548.0 42.3 %while.28 = (s32[]{:T(128)}, f32[1024,128]{1,0:T(8,128)}, f32[1024,128]{1,0:T(8,128)}, bf16[2,512,3,128]{3,1,2,0:T(8,128)(2,1)}, s32[2]{0:T(128)S(1)}, /*index=5...) while((s32[]{:T(128)}, f32[1024,128]{1,0:T(8,128)}, ...), condition=%wide.region_10.11_spmd.clone, body=%wide.region_8.10_spmd.clone.sunk | while | flops 2038234112 | bytes 91276160 | solution.py:126
  562.9 6.0 fusion.117
  584.1 6.1 fusion.117
  593.1 5.4 all-to-all-start.6
  602.8 5.0 all-to-all-start.7
  610.5 5.4 reduce.5
  622.3 9.0 all-to-all-done.5
  637.7 4.7 convolution_convert_fusion
  642.8 117.1 %reduce-scatter.6.cloned.1.call-done = bf16[192,2048]{1,0:T(8,128)(2,1)} async-done(((bf16[1536,2048]{1,0:T(8,128)(2,1)}), bf16[192,2048]{1,0:T(8,128)(2,1)}) %reduce-scatter.6.cloned.1.call-update) | async-done | bytes 786448 | tf_op jit(solution)/shard_map/reduce_scatter | solution.py:608
  761.6 6.1 fusion.56
  767.7 35.3 %all-reduce.5 = (bf16[1536]{0:T(1024)(128)(2,1)S(1)}, bf16[2048]{0:T(1024)(128)(2,1)S(1)}, bf16[1536]{0:T(1024)(128)(2,1)S(1)}) all-reduce(bf16[1536]{0:T(1024)(128)(2,1)S(1)} %get-tuple-element.220, bf16[2048]{0:T(1024)(128)(2,1)S(1)} %fusion.71, ...), channel_id=3, replica_groups=mesh['seq'=4,'fsdp'=8] {'fsdp'}, use_global_device_ids=true, to_apply=%region_15.16.clone | all-reduce | flops 5120 | bytes 20480
  803.2 6.5 all-reduce.7
  814.4 154.7 %all-reduce.11.cloned.1.call-done = (bf16[192,2048]{1,0:T(8,128)(2,1)}, bf16[192,1536]{1,0:T(8,128)(2,1)}, bf16[1120,1536]{1,0:T(8,128)(2,1)}, bf16[1120,1536]{1,0:T(8,128)(2,1)}, bf16[1120,1536]{1,0:T(8,128)(2,1)}) async-done(((bf16[192,2048]{1,0:T(8,128)(2,1)}, bf16[192,1536]{1,0:T(8,128)(2,1)}, bf16[1120,1536]{1,0:T(8,128)(2,1)}, bf16[1120,1536]{1,0:T(8,128)(2,1)}, bf16[1120,1536]{1,0:T(8,128)(2,1)}), ...) | async-done | bytes 11698192 | tf_op jit(solution)/shard_map/psum | solution.py:623
  969.1 6.0 convert_element_type.239
  (243 shorter events, 132.2 us)
Async XLA Ops:
  7.2 103.9 %copy-start.10 = (bf16[1,256,1536]{2,1,0:T(8,128)(2,1)S(1)}, bf16[1,256,1536]{2,1,0:T(8,128)(2,1)}, u32[]{:S(2)}) copy-start(bf16[1,256,1536]{2,1,0:T(8,128)(2,1)} %param.15) | copy-start | bytes 2359300
  7.2 29.1 %copy-start.40 = (bf16[256]{0:T(256)(128)(2,1)S(1)}, bf16[256]{0:T(256)(128)(2,1)}, u32[]{:S(2)}) copy-start(bf16[256]{0:T(256)(128)(2,1)} %param.19) | copy-start | bytes 1540
  7.2 45.7 %copy-start.39 = (s32[1,256]{1,0:T(1,128)S(1)}, s32[1,256]{1,0:T(1,128)}, u32[]{:S(2)}) copy-start(s32[1,256]{1,0:T(1,128)} %param.16) | copy-start | bytes 3076
  7.2 103.9 %all-gather.4.cloned.1.call-start = ((), (), s32[]{:S(2)}) async-start(), calls=%async_computation.11 | async-start | bytes 7077888 | tf_op jit(solution)/shard_map/all_gather | solution.py:482
  7.9 201.5 %all-gather.6.cloned.1.call-start = ((), (), s32[]{:S(2)}) async-start(), calls=%async_computation.12 | async-start | bytes 5308416 | tf_op jit(solution)/shard_map/all_gather | solution.py:484
  34.9 80.9 %copy-start.35 = (f32[1536]{0:T(1024)}, f32[1536]{0:T(1024)S(1)}, u32[]{:S(2)}) copy-start(f32[1536]{0:T(1024)S(1)} %convert_element_type.197) | copy-start | bytes 18436
  36.3 79.5 %copy-start.37 = (f32[256]{0:T(256)}, f32[256]{0:T(256)S(1)}, u32[]{:S(2)}) copy-start(f32[256]{0:T(256)S(1)} %add_rsqrt_fusion.1) | copy-start | bytes 3076
  53.5 68.0 %copy-start.23 = (f32[256,128]{1,0:T(8,128)}, f32[256,128]{1,0:T(8,128)S(1)}, u32[]{:S(2)}) copy-start(f32[256,128]{1,0:T(8,128)S(1)} %get-tuple-element.284) | copy-start | bytes 393220
  53.5 68.0 %copy-start.25 = (f32[256,128]{1,0:T(8,128)}, f32[256,128]{1,0:T(8,128)S(1)}, u32[]{:S(2)}) copy-start(f32[256,128]{1,0:T(8,128)S(1)} %get-tuple-element.283) | copy-start | bytes 393220
  53.6 73.8 %copy-start.27 = (f32[256,128]{0,1:T(8,128)}, f32[256,128]{0,1:T(8,128)S(1)}, u32[]{:S(2)}) copy-start(f32[256,128]{0,1:T(8,128)S(1)} %copy.95) | copy-start | bytes 393220
  123.3 8.3 all-to-all-start.1
  131.7 15.1 %all-to-all-start = ((bf16[256,4,384]{0,2,1:T(8,128)(2,1)}), bf16[256,4,384]{0,2,1:T(8,128)(2,1)S(1)}, u32[]{:S(2)}, u32[]{:S(2)}) async-start(bf16[256,4,384]{0,2,1:T(8,128)(2,1)} %fusion.59), calls=%async_computation | async-start | bytes 1572864 | tf_op jit(solution)/shard_map/all_to_all | solution.py:505
  147.5 9.7 all-to-all-start.2
  191.1 15.1 %all-to-all-start.3 = ((bf16[4,2,49152]{2,1,0:T(2,128)(2,1)}), bf16[4,2,49152]{2,1,0:T(2,128)(2,1)S(1)}, u32[]{:S(2)}, u32[]{:S(2)}) async-start(bf16[4,2,49152]{2,1,0:T(2,128)(2,1)} %reshape.322), calls=%async_computation.3 | async-start | bytes 1572864 | tf_op jit(solution)/shard_map/all_to_all | solution.py:513
  196.2 325.9 %reduce-scatter.4.cloned.1.call-start = ((), (), s32[]{:S(2)}) async-start(), calls=%async_computation.13 | async-start | bytes 7077888 | tf_op jit(solution)/shard_map/reduce_scatter | solution.py:530
  525.3 10.4 %copy-start.12 = (f32[256,1536]{1,0:T(8,128)}, f32[256,1536]{1,0:T(8,128)S(1)}, u32[]{:S(2)}) copy-start(f32[256,1536]{1,0:T(8,128)S(1)} %get-tuple-element.275) | copy-start | bytes 4718596
  529.7 6.1 copy-start.9
  530.8 14.8 %all-to-all-start.4 = ((bf16[256,4,384]{0,2,1:T(8,128)(2,1)}), bf16[256,4,384]{0,2,1:T(8,128)(2,1)}, u32[]{:S(2)}, u32[]{:S(2)}) async-start(bf16[256,4,384]{0,2,1:T(8,128)(2,1)} %bitcast.32), calls=%async_computation.5 | async-start | bytes 1572864 | tf_op jit(solution)/shard_map/all_to_all | solution.py:541
  535.5 107.2 %reduce-scatter.8.cloned.1.call-start = ((), (), s32[]{:S(2)}) async-start(), calls=%async_computation.15 | async-start | bytes 5308416 | tf_op jit(solution)/shard_map/reduce_scatter | solution.py:614
  539.4 8.6 copy-start.4
  539.4 8.6 copy-start.17
  562.9 6.0 copy-start.15
  562.9 6.0 copy-start.18
  584.1 6.1 copy-start.15
  584.1 6.1 copy-start.18
  593.1 9.7 all-to-all-start.6
  602.8 15.0 %all-to-all-start.7 = ((bf16[4,2,16384]{2,1,0:T(2,128)(2,1)}), bf16[4,2,16384]{2,1,0:T(2,128)(2,1)S(1)}, u32[]{:S(2)}, u32[]{:S(2)}) async-start(bf16[4,2,16384]{2,1,0:T(2,128)(2,1)} %reshape.324), calls=%async_computation.8 | async-start | bytes 524288 | tf_op jit(solution)/shard_map/all_to_all | solution.py:570
  617.8 13.5 %all-to-all-start.5 = ((bf16[4,2,49152]{2,1,0:T(2,128)(2,1)}), bf16[4,2,49152]{2,1,0:T(2,128)(2,1)S(1)}, u32[]{:S(2)}, u32[]{:S(2)}) async-start(bf16[4,2,49152]{2,1,0:T(2,128)(2,1)} %reshape.328), calls=%async_computation.6 | async-start | bytes 1572864 | tf_op jit(solution)/shard_map/all_to_all | solution.py:556
  621.3 138.5 %reduce-scatter.6.cloned.1.call-start = ((), (), s32[]{:S(2)}) async-start(), calls=%async_computation.14 | async-start | bytes 7077888 | tf_op jit(solution)/shard_map/reduce_scatter | solution.py:608
  642.4 326.6 %all-reduce.11.cloned.1.call-start = ((), (), s32[]{:S(2)}) async-start(), calls=%async_computation.16 | async-start | bytes 23396352 | tf_op jit(solution)/shard_map/psum | solution.py:623
  761.5 49.9 %copy-start.13 = (f32[256,1536]{1,0:T(8,128)S(1)}, f32[256,1536]{1,0:T(8,128)}, u32[]{:S(2)}) copy-start(f32[256,1536]{1,0:T(8,128)} %copy-done.12) | copy-start | bytes 4718596
  969.1 6.0 copy-start.21
  (31 other events, 87.4 us)
Sparse Core Ops, SparseCore 0:
  10.2 100.8 all-gather.3
  113.3 78.0 all-gather.5
  405.1 116.9 reduce-scatter.3
  540.3 94.3 reduce-scatter.7
  642.5 117.2 reduce-scatter.5
  762.7 206.2 all-reduce.10

commit v2 on v0

--- a/solution.py
+++ b/solution.py
@@ -1,8 +1,11 @@
+import functools
 import math
 
 import jax
 import jax.numpy as jnp
 from jax import lax
+from jax.experimental import pallas as pl
+from jax.experimental.pallas import tpu as pltpu
 from jax.sharding import PartitionSpec as P
 
 HEADS = 12
@@ -126,7 +129,954 @@
     return (grad_query.reshape(queries.shape), grad_keys, grad_values)
 
 
-def per_device(
+MESH = pl.DeviceIdType.MESH
+VMEM_BYTES = 67_000_000
+NN = (((1,), (0,)), ((), ()))
+NT = (((1,), (1,)), ((), ()))
+TN = (((0,), (0,)), ((), ()))
+
+
+def matmul(left, right, dims):
+    return lax.dot_general(left, right, dims, preferred_element_type=jnp.float32)
+
+
+def ring_place(index, size):
+    side = index % 2
+    return (index // 2) * (1 - side) + (size - 1 - index // 2) * side
+
+
+def ring_member(place, size):
+    side = place // (size // 2)
+    return 2 * (place * (1 - side) + (size - 1 - place) * side) + side
+
+
+def seq_partners(seq):
+    core = seq + 1 - 2 * (seq % 2)
+    far = (seq + 2) % 4
+    return core, far, (core + 2) % 4
+
+
+def greet(targets):
+    barrier = pltpu.get_barrier_semaphore()
+    for target in targets:
+        pl.semaphore_signal(barrier, inc=1, device_id=target, device_id_type=MESH)
+    pl.semaphore_wait(barrier, len(targets))
+
+
+def for_blocks(width, block, body):
+    @pl.loop(0, width // block)
+    def _(at):
+        body(pl.ds(pl.multiple_of(at * block, block), block))
+
+    if width % block:
+        body(pl.ds(width - width % block, width % block))
+
+
+def gather_kernel(
+    size,
+    rows_ref,
+    trig_ref,
+    piece_ref,
+    small_ref,
+    rows_out,
+    trig_out,
+    piece_out,
+    proj_out,
+    small_out,
+    rows_all,
+    trig_all,
+    pieces,
+    proj,
+    smalls,
+    load_sems,
+    store_sems,
+    ring_send,
+    ring_recv,
+    small_send,
+    small_recv,
+    seq_send,
+    seq_recv,
+    proj_send,
+    proj_recv,
+):
+    depth, joint = piece_ref.shape
+    half = depth // 2
+    group_width = proj.shape[0]
+    cut = joint - group_width
+    per_group = group_width // depth
+    me = lax.axis_index("fsdp")
+    seq = lax.axis_index("seq")
+    place = ring_place(me, size)
+    right = ring_member((place + 1) % size, size)
+    left = ring_member((place + size - 1) % size, size)
+    core, far, diagonal = seq_partners(seq)
+    sides = ((right, pl.ds(0, half)), (left, pl.ds(half, half)))
+
+    loads = [
+        pltpu.make_async_copy(piece_ref, pieces.at[me], load_sems.at[0]),
+        pltpu.make_async_copy(rows_ref, rows_all.at[seq], load_sems.at[1]),
+        pltpu.make_async_copy(trig_ref, trig_all.at[seq], load_sems.at[2]),
+        pltpu.make_async_copy(small_ref, smalls.at[me], load_sems.at[3]),
+    ]
+    for load in loads:
+        load.start()
+    greet(({"fsdp": right}, {"fsdp": left}, {"seq": core}, {"seq": far}, {"seq": diagonal}))
+
+    def piece_of(step, side):
+        return ring_member((place + size - step if side == 0 else place + step) % size, size)
+
+    def ring_copy(step, side):
+        target, span = sides[side]
+        at = piece_of(step, side)
+        return pltpu.make_async_remote_copy(
+            src_ref=pieces.at[at, span],
+            dst_ref=pieces.at[at, span],
+            send_sem=ring_send.at[side, step],
+            recv_sem=ring_recv.at[side, step],
+            device_id={"fsdp": target},
+            device_id_type=MESH,
+        )
+
+    def small_copy(step):
+        at = piece_of(step, 0)
+        return pltpu.make_async_remote_copy(
+            src_ref=smalls.at[at],
+            dst_ref=smalls.at[at],
+            send_sem=small_send.at[step],
+            recv_sem=small_recv.at[step],
+            device_id={"fsdp": right},
+            device_id_type=MESH,
+        )
+
+    def seq_copy(which, block, target, at):
+        held = (rows_all, trig_all)[which]
+        return pltpu.make_async_remote_copy(
+            src_ref=held.at[block],
+            dst_ref=held.at[block],
+            send_sem=seq_send.at[which, at],
+            recv_sem=seq_recv.at[which, at],
+            device_id={"seq": target},
+            device_id_type=MESH,
+        )
+
+    def proj_part(step, side):
+        at = piece_of(step, side)
+        owner = at // per_group
+        row = pl.multiple_of((at % per_group) * depth + side * half, half)
+        source = pieces.at[at, pl.ds(side * half, half), pl.ds(cut, group_width)]
+        target = proj.at[pl.ds(row, half), pl.ds(pl.multiple_of(seq * group_width, 128), group_width)]
+        return at, owner, source, target
+
+    def proj_copy(step, side):
+        at, owner, source, target = proj_part(step, side)
+        return owner, pltpu.make_async_remote_copy(
+            src_ref=source,
+            dst_ref=target,
+            send_sem=proj_send.at[side, step],
+            recv_sem=proj_recv.at[seq, at % per_group, side],
+            device_id={"seq": owner},
+            device_id_type=MESH,
+        )
+
+    def proj_start(step, side):
+        owner, copy = proj_copy(step, side)
+
+        @pl.when(owner != seq)
+        def _():
+            copy.start()
+
+        @pl.when(owner == seq)
+        def _():
+            _, _, source, target = proj_part(step, side)
+            pltpu.make_async_copy(source, target, proj_send.at[side, step]).start()
+
+    loads[0].wait()
+    for side in range(2):
+        ring_copy(0, side).start()
+    loads[3].wait()
+    small_copy(0).start()
+    for which in (1, 0):
+        loads[1 + which].wait()
+        seq_copy(which, seq, far, 1).start()
+        seq_copy(which, seq, core, 0).start()
+    for side in range(2):
+        proj_start(0, side)
+
+    for step in range(size - 1):
+        for side in range(2):
+            ring_copy(step, side).wait_recv()
+            if step < size - 2:
+                ring_copy(step + 1, side).start()
+        small_copy(step).wait_recv()
+        if step < size - 2:
+            small_copy(step + 1).start()
+        for side in range(2):
+            proj_start(step + 1, side)
+        if step == min(1, size - 2):
+            for which in (1, 0):
+                seq_copy(which, seq, far, 1).wait_recv()
+                seq_copy(which, far, core, 2).start()
+
+    store_pieces = pltpu.make_async_copy(pieces, piece_out, store_sems.at[0])
+    store_small = pltpu.make_async_copy(smalls, small_out, store_sems.at[1])
+    store_pieces.start()
+    store_small.start()
+    for which in (1, 0):
+        seq_copy(which, seq, core, 0).wait_recv()
+        seq_copy(which, far, core, 2).wait_recv()
+    store_rows = pltpu.make_async_copy(rows_all, rows_out, store_sems.at[2])
+    store_trig = pltpu.make_async_copy(trig_all, trig_out, store_sems.at[3])
+    store_rows.start()
+    store_trig.start()
+    for peer in (core, far, diagonal):
+        for at in range(per_group):
+            for side in range(2):
+                pltpu.make_async_remote_copy(
+                    src_ref=pieces.at[0, pl.ds(0, half), pl.ds(cut, group_width)],
+                    dst_ref=proj.at[pl.ds(0, half), pl.ds(0, group_width)],
+                    send_sem=proj_send.at[side, 0],
+                    recv_sem=proj_recv.at[peer, at, side],
+                    device_id={"seq": peer},
+                    device_id_type=MESH,
+                ).wait_recv()
+    for step in range(size):
+        for side in range(2):
+            owner, copy = proj_copy(step, side)
+
+            @pl.when(owner != seq)
+            def _():
+                copy.wait_send()
+
+            @pl.when(owner == seq)
+            def _():
+                _, _, source, target = proj_part(step, side)
+                pltpu.make_async_copy(source, target, proj_send.at[side, step]).wait()
+
+    store_proj = pltpu.make_async_copy(proj, proj_out, store_sems.at[4])
+    store_proj.start()
+    for step in range(size - 1):
+        for side in range(2):
+            ring_copy(step, side).wait_send()
+        small_copy(step).wait_send()
+    for which in (1, 0):
+        seq_copy(which, seq, core, 0).wait_send()
+        seq_copy(which, seq, far, 1).wait_send()
+        seq_copy(which, far, core, 2).wait_send()
+    for store in (store_pieces, store_small, store_rows, store_trig, store_proj):
+        store.wait()
+
+
+def gather_inputs(rows, trig, piece, small):
+    size = lax.axis_size("fsdp")
+    groups = lax.axis_size("seq")
+    tokens, width = rows.shape
+    depth, joint = piece.shape
+    group_width = width // groups
+    f32, bf16 = jnp.float32, jnp.bfloat16
+    shapes = (
+        ((groups, tokens, width), bf16),
+        ((groups,) + trig.shape, f32),
+        ((size, depth, joint), bf16),
+        ((group_width, width), bf16),
+        ((size,) + small.shape, bf16),
+    )
+    dma = pltpu.SemaphoreType.DMA
+    anywhere = pl.BlockSpec(memory_space=pl.ANY)
+    per_group = group_width // depth
+    return pl.pallas_call(
+        functools.partial(gather_kernel, size),
+        out_shape=tuple(jax.ShapeDtypeStruct(*shape) for shape in shapes),
+        in_specs=[anywhere] * 4,
+        out_specs=(anywhere,) * 5,
+        scratch_shapes=[pltpu.VMEM(*shape) for shape in shapes]
+        + [
+            dma((4,)),
+            dma((5,)),
+            dma((2, size)),
+            dma((2, size)),
+            dma((size,)),
+            dma((size,)),
+            dma((2, 3)),
+            dma((2, 3)),
+            dma((2, size)),
+            dma((groups, per_group, 2)),
+        ],
+        compiler_params=pltpu.CompilerParams(
+            collective_id=1, has_side_effects=True, vmem_limit_bytes=32_000_000
+        ),
+        name="gather_inputs",
+    )(rows, trig, piece, small)
+
+
+def turn_tables(trig):
+    lane = lax.broadcasted_iota(jnp.int32, trig.shape, 1)
+    swapped = pltpu.roll(trig, HEAD_DIM // 2, 1)
+    first = lane < HEAD_DIM // 2
+    return jnp.where(first, trig, swapped), jnp.where(first, -swapped, trig)
+
+
+def head_columns(at):
+    return slice(at * HEAD_DIM, (at + 1) * HEAD_DIM)
+
+
+def causal(scores, start):
+    rows = lax.broadcasted_iota(jnp.int32, scores.shape, 0) + start
+    columns = lax.broadcasted_iota(jnp.int32, scores.shape, 1)
+    return jnp.where(columns <= rows, scores, -1e30)
+
+
+def attend_forward_kernel(
+    block,
+    rows_ref,
+    weight_ref,
+    proj_ref,
+    trig_ref,
+    gain_ref,
+    bias_ref,
+    normed_ref,
+    heads_ref,
+    out_ref,
+    log_ref,
+    part_ref,
+):
+    length = rows_ref.shape[0]
+    used = heads_ref.shape[1]
+    count = used // HEAD_DIM - 2
+    scale = HEAD_DIM**-0.5
+    for start in range(0, length, block):
+        span = slice(start, start + block)
+        rows = rows_ref[span, :].astype(jnp.float32)
+        inverse = lax.rsqrt(jnp.mean(rows * rows, axis=-1, keepdims=True) + norm_eps)
+        normed_ref[span, :] = (rows * inverse * gain_ref[...]).astype(jnp.bfloat16)
+        mixed = matmul(normed_ref[span, :], weight_ref[:, :used], NN) + bias_ref[...]
+        cosine, sine = turn_tables(trig_ref[span, :])
+        for at in range(count + 1):
+            part = mixed[:, head_columns(at)]
+            turned = pltpu.roll(part, HEAD_DIM // 2, 1)
+            heads_ref[span, head_columns(at)] = (part * cosine + turned * sine).astype(
+                jnp.bfloat16
+            )
+        heads_ref[span, head_columns(count + 1)] = mixed[:, head_columns(count + 1)].astype(
+            jnp.bfloat16
+        )
+    lane = lax.broadcasted_iota(jnp.int32, (block, HEAD_DIM), 1)
+    for start in range(0, length, block):
+        span = slice(start, start + block)
+        seen = slice(0, start + block)
+        logs = jnp.zeros((block, HEAD_DIM), jnp.float32)
+        for at in range(count):
+            scores = causal(
+                matmul(heads_ref[span, head_columns(at)], heads_ref[seen, head_columns(count)], NT)
+                * scale,
+                start,
+            )
+            top = jnp.max(scores, axis=-1, keepdims=True)
+            exponent = jnp.exp(scores - top)
+            total = jnp.sum(exponent, axis=-1, keepdims=True)
+            probability = (exponent / total).astype(jnp.bfloat16)
+            out_ref[span, head_columns(at)] = matmul(
+                probability, heads_ref[seen, head_columns(count + 1)], NN
+            ).astype(jnp.bfloat16)
+            logs = jnp.where(lane == at, top + jnp.log(total), logs)
+        log_ref[span, :] = logs
+        part_ref[span, :] = matmul(out_ref[span, :], proj_ref[...], NN).astype(jnp.bfloat16)
+
+
+def attend_group(rows, weight, proj, trig, gain, bias):
+    length, width = rows.shape
+    used = bias.shape[1]
+    own = proj.shape[0]
+    bf16 = jnp.bfloat16
+    inside = pl.BlockSpec(memory_space=pltpu.VMEM)
+    return pl.pallas_call(
+        functools.partial(attend_forward_kernel, 256),
+        out_shape=(
+            jax.ShapeDtypeStruct((length, width), bf16),
+            jax.ShapeDtypeStruct((length, used), bf16),
+            jax.ShapeDtypeStruct((length, own), bf16),
+            jax.ShapeDtypeStruct((length, HEAD_DIM), jnp.float32),
+            jax.ShapeDtypeStruct((length, width), bf16),
+        ),
+        in_specs=[inside] * 6,
+        out_specs=(inside,) * 5,
+        compiler_params=pltpu.CompilerParams(vmem_limit_bytes=VMEM_BYTES),
+        cost_estimate=pl.CostEstimate(
+            flops=2 * length * width * (used + own) + 4 * length * length * own,
+            bytes_accessed=2 * (3 * length * width + 2 * width * width),
+            transcendentals=length * length * own // HEAD_DIM,
+        ),
+        name="attend_forward",
+    )(rows, weight, proj, trig, gain, bias)
+
+
+def mlp_kernel(
+    size,
+    hidden_ref,
+    part_ref,
+    gain_ref,
+    cots_ref,
+    gate_ref,
+    up_ref,
+    down_ref,
+    outs_ref,
+    resid_ref,
+    proj_grads_ref,
+    back_ref,
+    gain_grad_ref,
+    sums_ref,
+    rows_all,
+    cots,
+    weights,
+    grads,
+    hid,
+    dgate,
+    dup,
+    partial,
+    resid,
+    sums_in,
+    sums_out,
+    outs,
+    seq_in,
+    seq_own,
+    load_sems,
+    cot_sems,
+    ring_send,
+    ring_recv,
+    sum_send,
+    sum_recv,
+    out_sems,
+    seq_send,
+    seq_recv,
+    swap_send,
+    swap_recv,
+    swap_ready,
+):
+    tokens, width = hidden_ref.shape
+    units = gate_ref.shape[0]
+    half = tokens // 2
+    me = lax.axis_index("fsdp")
+    seq = lax.axis_index("seq")
+    place = ring_place(me, size)
+    right = ring_member((place + 1) % size, size)
+    left = ring_member((place + size - 1) % size, size)
+    core, far, diagonal = seq_partners(seq)
+    sides = ((right, pl.ds(0, half)), (left, pl.ds(half, half)))
+
+    def owner_of(step, side):
+        return ring_member((place + size - step if side == 0 else place + step) % size, size)
+
+    def part_rows(block):
+        return part_ref.at[pl.ds(pl.multiple_of(block * tokens, tokens), tokens)]
+
+    part_loads = [
+        pltpu.make_async_copy(part_rows(far), seq_own.at[0], load_sems.at[3]),
+        pltpu.make_async_copy(part_rows(seq), seq_own.at[1], load_sems.at[4]),
+        pltpu.make_async_copy(hidden_ref, seq_own.at[2], load_sems.at[5]),
+    ]
+    weight_loads = [
+        pltpu.make_async_copy(ref, weights.at[at], load_sems.at[at])
+        for at, ref in enumerate((gate_ref, up_ref, down_ref))
+    ]
+    for load in part_loads:
+        load.start()
+    greet(({"fsdp": right}, {"fsdp": left}, {"seq": core}, {"seq": far}))
+
+    def seq_copy(at, source, target):
+        return pltpu.make_async_remote_copy(
+            src_ref=source,
+            dst_ref=seq_in.at[at],
+            send_sem=seq_send.at[at],
+            recv_sem=seq_recv.at[at],
+            device_id={"seq": target},
+            device_id_type=MESH,
+        )
+
+    core_copies = [seq_copy(0, part_rows(diagonal), core), seq_copy(1, part_rows(core), core)]
+    far_copy = seq_copy(2, sums_out.at[0], far)
+    for copy in core_copies:
+        copy.start()
+
+    def cot_copies(step):
+        return [
+            pltpu.make_async_copy(
+                cots_ref.at[
+                    pl.ds(
+                        pl.multiple_of(owner_of(step, side) * tokens + side * half, half), half
+                    )
+                ],
+                cots.at[step % 2, sides[side][1]],
+                cot_sems.at[step % 2, side],
+            )
+            for side in range(2)
+        ]
+
+    for load in weight_loads + cot_copies(0):
+        load.start()
+
+    @pl.loop(0, units // 16)
+    def _(at):
+        zeros = jnp.zeros((3, 16, width), jnp.float32)
+        grads[:, pl.ds(pl.multiple_of(at * 16, 16), 16), :] = zeros
+
+    part_loads[0].wait()
+    core_copies[0].wait_recv()
+    sums_out[0] = (seq_own[0].astype(jnp.float32) + seq_in[0].astype(jnp.float32)).astype(
+        jnp.bfloat16
+    )
+    far_copy.start()
+    part_loads[1].wait()
+    part_loads[2].wait()
+    core_copies[1].wait_recv()
+    resid[...] = (
+        seq_own[1].astype(jnp.float32)
+        + seq_in[1].astype(jnp.float32)
+        + seq_own[2].astype(jnp.float32)
+    )
+    far_copy.wait_recv()
+    resid[...] += seq_in[2].astype(jnp.float32)
+
+    def inverse_of(values):
+        return lax.rsqrt(jnp.mean(values * values, axis=-1, keepdims=True) + norm_eps)
+
+    rows_all[0] = (resid[...] * inverse_of(resid[...]) * gain_ref[...]).astype(jnp.bfloat16)
+    far_copy.wait_send()
+    resid_store = pltpu.make_async_copy(resid, resid_ref, load_sems.at[6])
+    resid_store.start()
+
+    def row_copy(step, side):
+        target, span = sides[side]
+        return pltpu.make_async_remote_copy(
+            src_ref=rows_all.at[step, span],
+            dst_ref=rows_all.at[step + 1, span],
+            send_sem=ring_send.at[side, step],
+            recv_sem=ring_recv.at[side, step + 1],
+            device_id={"fsdp": target},
+            device_id_type=MESH,
+        )
+
+    def sum_copy(step, side):
+        target, span = sides[side]
+        return pltpu.make_async_remote_copy(
+            src_ref=sums_out.at[step % 2, span],
+            dst_ref=sums_in.at[step, span],
+            send_sem=sum_send.at[side, step],
+            recv_sem=sum_recv.at[side, step],
+            device_id={"fsdp": target},
+            device_id_type=MESH,
+        )
+
+    def out_copy(step, side):
+        at = pl.multiple_of(owner_of(step, side) * tokens + side * half, half)
+        return pltpu.make_async_copy(
+            outs.at[step % 2, sides[side][1]], outs_ref.at[pl.ds(at, half)], out_sems.at[side, step]
+        )
+
+    def elementwise(step, span):
+        rows = rows_all[step]
+        gate = matmul(rows, weights[0, span, :], NT)
+        up = matmul(rows, weights[1, span, :], NT)
+        grad_hidden = matmul(cots[step % 2], weights[2, span, :], NT)
+        sigmoid = jax.nn.sigmoid(gate)
+        activated = gate * sigmoid
+        hid[:, span] = (activated * up).astype(jnp.bfloat16)
+        dgate[:, span] = (
+            grad_hidden * up * sigmoid * (1.0 + gate * (1.0 - sigmoid))
+        ).astype(jnp.bfloat16)
+        dup[:, span] = (grad_hidden * activated).astype(jnp.bfloat16)
+
+    for load in weight_loads:
+        load.wait()
+
+    @pl.loop(0, size)
+    def _(step):
+        slot = step % 2
+
+        @pl.when(step >= 1)
+        def _():
+            for side in range(2):
+                row_copy(step - 1, side).wait_recv()
+
+        @pl.when(step < size - 1)
+        def _():
+            for side in range(2):
+                row_copy(step, side).start()
+
+        for load in cot_copies(step):
+            load.wait()
+
+        @pl.when(step < size - 1)
+        def _():
+            for load in cot_copies(step + 1):
+                load.start()
+
+        for_blocks(units, 256, functools.partial(elementwise, step))
+
+        def back_part(span):
+            partial[:, span] = matmul(dgate[...], weights[0, :, span], NN) + matmul(
+                dup[...], weights[1, :, span], NN
+            )
+
+        for_blocks(width, 256, back_part)
+
+        @pl.when(step == 0)
+        def _():
+            back_ref[...] = partial[...]
+
+        @pl.when(step >= 3)
+        def _():
+            for side in range(2):
+                sum_copy(step - 2, side).wait_send()
+
+        @pl.when(step == 1)
+        def _():
+            sums_out[slot] = partial[...].astype(jnp.bfloat16)
+
+        @pl.when(step >= 2)
+        def _():
+            for side in range(2):
+                sum_copy(step - 1, side).wait_recv()
+            sums_out[slot] = (partial[...] + sums_in[step - 1].astype(jnp.float32)).astype(
+                jnp.bfloat16
+            )
+
+        @pl.when(step >= 1)
+        def _():
+            for side in range(2):
+                sum_copy(step, side).start()
+
+        @pl.when(step >= 2)
+        def _():
+            for side in range(2):
+                out_copy(step - 2, side).wait()
+
+        def out_part(span):
+            outs[slot, :, span] = matmul(hid[...], weights[2, :, span], NN).astype(jnp.bfloat16)
+
+        for_blocks(width, 256, out_part)
+        for side in range(2):
+            out_copy(step, side).start()
+
+        def weight_part(span):
+            rows, cot = rows_all[step, :, span], cots[slot, :, span]
+            grads[0, :, span] += matmul(dgate[...], rows, TN)
+            grads[1, :, span] += matmul(dup[...], rows, TN)
+            grads[2, :, span] += matmul(hid[...], cot, TN)
+
+        for_blocks(width, 256, weight_part)
+
+    share = units // 2
+    kept = pl.multiple_of((seq % 2) * share, 16)
+    given = pl.multiple_of((1 - seq % 2) * share, 16)
+    pl.semaphore_signal(swap_ready, inc=1, device_id={"seq": core}, device_id_type=MESH)
+    swaps = [
+        pltpu.make_async_remote_copy(
+            src_ref=weights.at[at, pl.ds(given, share)],
+            dst_ref=weights.at[at, pl.ds(given, share)],
+            send_sem=swap_send.at[at],
+            recv_sem=swap_recv.at[at],
+            device_id={"seq": core},
+            device_id_type=MESH,
+        )
+        for at in range(3)
+    ]
+    for at in range(3):
+
+        @pl.loop(0, share // 16)
+        def _(block):
+            span = pl.ds(pl.multiple_of(given + block * 16, 16), 16)
+            weights[at, span, :] = grads[at, span, :].astype(jnp.bfloat16)
+
+        if at == 0:
+            pl.semaphore_wait(swap_ready, 1)
+        swaps[at].start()
+
+    for side in range(2):
+        sum_copy(size - 1, side).wait_recv()
+    grad_normed = back_ref[...] + sums_in[size - 1].astype(jnp.float32)
+    inverse = inverse_of(resid[...])
+    unit_rows = resid[...] * inverse
+    gain_grad_ref[...] = jnp.sum(grad_normed * unit_rows, axis=0, keepdims=True)
+    grad_unit = grad_normed * gain_ref[...]
+    cot_own = pltpu.make_async_copy(
+        cots_ref.at[pl.ds(pl.multiple_of(me * tokens, tokens), tokens)],
+        cots.at[0],
+        load_sems.at[7],
+    )
+    cot_own.start()
+    cot_own.wait()
+    back_ref[...] = cots[0].astype(jnp.float32) + inverse * (
+        grad_unit - unit_rows * jnp.mean(grad_unit * unit_rows, axis=-1, keepdims=True)
+    )
+    for side in range(2):
+        sum_copy(size - 2, side).wait_send()
+        sum_copy(size - 1, side).wait_send()
+    sums_out[0] = back_ref[...].astype(jnp.bfloat16)
+
+    def grad_copy(source, block, target, at):
+        return pltpu.make_async_remote_copy(
+            src_ref=source,
+            dst_ref=proj_grads_ref.at[block],
+            send_sem=seq_send.at[at],
+            recv_sem=seq_recv.at[at],
+            device_id={"seq": target},
+            device_id_type=MESH,
+        )
+
+    to_far = grad_copy(sums_out.at[0], seq, far, 3)
+    to_core = grad_copy(sums_out.at[0], seq, core, 4)
+    passed_on = grad_copy(proj_grads_ref.at[far], far, core, 5)
+    keep = pltpu.make_async_copy(sums_out.at[0], proj_grads_ref.at[seq], load_sems.at[8])
+    to_far.start()
+    to_core.start()
+    keep.start()
+    stores = []
+    for at in range(3):
+        swaps[at].wait_recv()
+
+        @pl.loop(0, share // 16)
+        def _(block):
+            span = pl.ds(pl.multiple_of(kept + block * 16, 16), 16)
+            weights[at, span, :] = (
+                grads[at, span, :] + weights[at, span, :].astype(jnp.float32)
+            ).astype(jnp.bfloat16)
+
+        stores.append(
+            pltpu.make_async_copy(
+                weights.at[at, pl.ds(kept, share)], sums_ref.at[at], load_sems.at[at]
+            )
+        )
+        stores[-1].start()
+    to_far.wait_recv()
+    passed_on.start()
+    for side in range(2):
+        out_copy(size - 2, side).wait()
+        out_copy(size - 1, side).wait()
+
+        @pl.loop(0, size - 1)
+        def _(step):
+            row_copy(step, side).wait_send()
+
+    for copy in core_copies + swaps + [to_far, to_core, passed_on]:
+        copy.wait_send()
+    to_core.wait_recv()
+    passed_on.wait_recv()
+    for store in stores + [keep, resid_store]:
+        store.wait()
+
+
+def mlp_ring(hidden, part, gain, cots, gate_weight, up_weight, down_weight):
+    size = lax.axis_size("fsdp")
+    groups = lax.axis_size("seq")
+    tokens, width = hidden.shape
+    units = gate_weight.shape[0]
+    anywhere = pl.BlockSpec(memory_space=pl.ANY)
+    inside = pl.BlockSpec(memory_space=pltpu.VMEM)
+    bf16, f32 = jnp.bfloat16, jnp.float32
+    dma = pltpu.SemaphoreType.DMA
+    return pl.pallas_call(
+        functools.partial(mlp_kernel, size),
+        out_shape=(
+            jax.ShapeDtypeStruct((size * tokens, width), bf16),
+            jax.ShapeDtypeStruct((tokens, width), f32),
+            jax.ShapeDtypeStruct((groups, tokens, width), bf16),
+            jax.ShapeDtypeStruct((tokens, width), f32),
+            jax.ShapeDtypeStruct((1, width), f32),
+            jax.ShapeDtypeStruct((3, units // 2, width), bf16),
+        ),
+        in_specs=[anywhere, anywhere, inside, anywhere, anywhere, anywhere, anywhere],
+        out_specs=(anywhere, anywhere, anywhere, inside, inside, anywhere),
+        scratch_shapes=[
+            pltpu.VMEM((size, tokens, width), bf16),
+            pltpu.VMEM((2, tokens, width), bf16),
+            pltpu.VMEM((3, units, width), bf16),
+            pltpu.VMEM((3, units, width), f32),
+            pltpu.VMEM((tokens, units), bf16),
+            pltpu.VMEM((tokens, units), bf16),
+            pltpu.VMEM((tokens, units), bf16),
+            pltpu.VMEM((tokens, width), f32),
+            pltpu.VMEM((tokens, width), f32),
+            pltpu.VMEM((size, tokens, width), bf16),
+            pltpu.VMEM((2, tokens, width), bf16),
+            pltpu.VMEM((2, tokens, width), bf16),
+            pltpu.VMEM((3, tokens, width), bf16),
+            pltpu.VMEM((3, tokens, width), bf16),
+            dma((9,)),
+            dma((2, 2)),
+            dma((2, size)),
+            dma((2, size)),
+            dma((2, size)),
+            dma((2, size)),
+            dma((2, size)),
+            dma((6,)),
+            dma((6,)),
+            dma((3,)),
+            dma((3,)),
+            pltpu.SemaphoreType.REGULAR,
+        ],
+        compiler_params=pltpu.CompilerParams(
+            collective_id=0, has_side_effects=True, vmem_limit_bytes=VMEM_BYTES
+        ),
+        name="mlp_ring",
+    )(hidden, part, gain, cots, gate_weight, up_weight, down_weight)
+
+
+def kernels_fit(hidden_in, positions, attn_gain, qkv_weight, qkv_bias, out_weight, *rest):
+    size, groups = lax.axis_size("fsdp"), lax.axis_size("seq")
+    _, tokens, width = hidden_in.shape
+    units = rest[1].shape[0]
+    if groups != 4 or size % 4 or tokens % 256 or units % 32 or width % 512:
+        return False
+    if (width // size) % 32 or qkv_bias.shape[0] > 256 or KV_HEADS != 2:
+        return False
+    rows = tokens * width * (4 * size + 34)
+    return rows + units * (18 * width + 6 * tokens) < 64_000_000
+
+
+def group_columns(array, seq):
+    width_query = HEADS * HEAD_DIM
+    own = width_query // 4
+    kv_head = seq // 2
+    parts = (
+        (seq * own, own),
+        (width_query + kv_head * HEAD_DIM, HEAD_DIM),
+        (width_query + (KV_HEADS + kv_head) * HEAD_DIM, HEAD_DIM),
+    )
+    return jnp.concatenate(
+        [lax.dynamic_slice_in_dim(array, at, count, array.ndim - 1) for at, count in parts], -1
+    )
+
+
+def per_device_kernels(
+    hidden_in,
+    positions,
+    attn_gain,
+    qkv_weight,
+    qkv_bias,
+    out_weight,
+    mlp_gain,
+    gate_weight,
+    up_weight,
+    down_weight,
+    cotangent,
+):
+    f32, bf16 = jnp.float32, jnp.bfloat16
+    groups = lax.axis_size("seq")
+    size = lax.axis_size("fsdp")
+    seq = lax.axis_index("seq")
+    _, tokens, width = hidden_in.shape
+    length = tokens * groups
+    own = width // groups
+    used = own + 2 * HEAD_DIM
+    all_cots = lax.all_gather(cotangent[0], "fsdp", axis=0, tiled=True)
+    cosine, sine = rope_tables(positions[0])
+    half_dim = HEAD_DIM // 2
+    trig = jnp.concatenate([cosine[:, :half_dim], sine[:, half_dim:]], axis=1)
+    piece = jnp.concatenate(
+        [
+            group_columns(qkv_weight, seq),
+            lax.dynamic_slice_in_dim(out_weight, seq * own, own, 1),
+        ],
+        axis=1,
+    )
+    small_width = 256
+    small = jnp.stack(
+        [
+            jnp.pad(row, (0, small_width - row.shape[0]))
+            for row in (attn_gain, mlp_gain, qkv_bias)
+        ]
+    )
+    small = jnp.pad(small, ((0, 13), (0, 0)))
+    rows_all, trig_all, pieces, proj, smalls = gather_inputs(hidden_in[0], trig, piece, small)
+    shard = width // size
+    gain_one = smalls[:, 0, :shard].reshape(1, width).astype(f32)
+    gain_two = smalls[:, 1, :shard].reshape(1, width).astype(f32)
+    bias = group_columns(smalls[:, 2, : qkv_bias.shape[0]].reshape(1, -1), seq).astype(f32)
+    rows_all = rows_all.reshape(length, width)
+    trig_all = trig_all.reshape(length, HEAD_DIM)
+    weight = pieces.reshape(width, piece.shape[1])
+    normed_one, heads, attended, logs, part = attend_group(
+        rows_all, weight, proj, trig_all, gain_one, bias
+    )
+    outs, residual, proj_grads, grad_residual, term_gain_two, unit_sums = mlp_ring(
+        hidden_in[0], part, gain_two, all_cots, gate_weight, up_weight, down_weight
+    )
+    mlp_out = lax.psum_scatter(outs, "fsdp", scatter_dimension=0, tiled=True).astype(f32)
+    hidden_out = (residual + mlp_out).astype(bf16)
+    proj_grads = proj_grads.reshape(length, width)
+
+    count = own // HEAD_DIM
+    grad_heads = jnp.einsum("td,ed->te", proj_grads, proj, preferred_element_type=f32).astype(bf16)
+    term_out = jnp.einsum("te,td->ed", attended, proj_grads, preferred_element_type=f32)
+    grad_query, grad_keys, grad_values = attend_backward(
+        heads[:, :own].reshape(length, count, HEAD_DIM),
+        heads[:, own : own + HEAD_DIM],
+        heads[:, own + HEAD_DIM :],
+        logs[:, :count].reshape(2, length // 2, count).transpose(0, 2, 1),
+        grad_heads.reshape(length, count, HEAD_DIM),
+    )
+    cosine_all = jnp.concatenate([trig_all[:, :half_dim]] * 2, axis=1)
+    sine_all = jnp.concatenate([trig_all[:, half_dim:]] * 2, axis=1)
+    grad_query = unrotate(grad_query.astype(bf16).astype(f32), cosine_all, sine_all)
+    grad_keys = unrotate(grad_keys.astype(bf16).astype(f32)[:, None], cosine_all, sine_all)[:, 0]
+    grad_mixed = jnp.concatenate(
+        [grad_query.reshape(length, own), grad_keys, grad_values.astype(bf16).astype(f32)], axis=1
+    ).astype(bf16)
+    term_qkv = jnp.einsum("td,tc->dc", normed_one, grad_mixed, preferred_element_type=f32)
+    term_bias = jnp.sum(grad_mixed.astype(f32), axis=0)
+    grad_normed = jnp.einsum(
+        "tc,dc->td", grad_mixed, weight[:, :used], preferred_element_type=f32
+    )
+    grad_normed = lax.psum_scatter(grad_normed.astype(bf16), "seq", scatter_dimension=0, tiled=True)
+    unit_one, inverse_one, _ = norm_forward(hidden_in[0].astype(f32), gain_one)
+    grad_norm_one, term_gain_one = norm_backward(
+        grad_normed.astype(f32), unit_one, inverse_one, gain_one
+    )
+    grad_rows = grad_residual + grad_norm_one
+
+    width_query = HEADS * HEAD_DIM
+
+    def spread(term):
+        full = jnp.zeros(term.shape[:-1] + (width_query + 2 * KV_HEADS * HEAD_DIM,), f32)
+        kv_head = seq // 2
+        full = lax.dynamic_update_slice_in_dim(full, term[..., :own], seq * own, term.ndim - 1)
+        full = lax.dynamic_update_slice_in_dim(
+            full, term[..., own : own + HEAD_DIM], width_query + kv_head * HEAD_DIM, term.ndim - 1
+        )
+        return lax.dynamic_update_slice_in_dim(
+            full,
+            term[..., own + HEAD_DIM :],
+            width_query + (KV_HEADS + kv_head) * HEAD_DIM,
+            term.ndim - 1,
+        )
+
+    def reduced(term):
+        shard_sum = lax.psum_scatter(
+            term.astype(bf16), "fsdp", scatter_dimension=0, tiled=True
+        )
+        return lax.psum(shard_sum, "seq").astype(f32)
+
+    full_out = lax.dynamic_update_slice_in_dim(jnp.zeros((width, width), f32), term_out, seq * own, 0)
+    far_sums = lax.ppermute(unit_sums, "seq", [(at, (at + 2) % 4) for at in range(4)])
+    totals = (unit_sums.astype(f32) + far_sums.astype(f32)).astype(bf16)
+    others = lax.ppermute(totals, "seq", [(at, at + 1 - 2 * (at % 2)) for at in range(4)])
+    first = jnp.where(seq % 2 == 0, totals, others)
+    second = jnp.where(seq % 2 == 0, others, totals)
+    units_grads = jnp.concatenate([first, second], axis=1).astype(f32)
+    return (
+        hidden_out[None],
+        grad_rows[None],
+        reduced(term_gain_one),
+        reduced(spread(term_qkv)),
+        reduced(spread(term_bias)),
+        reduced(full_out),
+        reduced(term_gain_two[0]),
+        units_grads[0],
+        units_grads[1],
+        units_grads[2],
+    )
+
+
+def per_device_gathered(
     hidden_in,
     positions,
     attn_gain,
@@ -330,6 +1280,10 @@
     )
 
 
+def per_device(*arguments):
+    return (per_device_kernels if kernels_fit(*arguments) else per_device_gathered)(*arguments)
+
+
 def solution(mesh):
     placed = (
         P("fsdp", "seq", None),

time: 1290 us -> 834 us (0.65)
  waiting for transfers between devices: 815 us -> 326 us
  Pallas kernels: 0 us -> 268 us
  matrix products: 191 us -> 49.4 us
  starting transfers between devices: 38.7 us -> 0.84 us
  blocking collectives: 80.7 us -> 45.7 us
    pallas_call x0 -> x3, Pallas kernels: none -> 268 us  [the longest x1 175 us: mlp_ring(): pl.pallas_call(functools.partial(mlp_kernel, size), out_shape=(jax.ShapeD...]
    reduce_scatter x4, waiting for transfers between devices: 396 us -> 151 us  [the longest x1 106 us: per_device_kernels(): lax.psum_scatter(outs, 'fsdp', scatter_dimension=0, tiled=True).astype(f32)]
    all_gather x4 -> x1, waiting for transfers between devices: 225 us -> 9.6 us  [per_device_kernels(): all_cots = lax.all_gather(cotangent[0], 'fsdp', axis=0, tiled=True)]
    dot_general x17 -> x4, matrix products: 150 us -> 16.1 us  [the longest x1 4.8 us: per_device_kernels(): jnp.einsum('td,tc->dc', normed_one, grad_mixed, preferred_element_type=f32)]
    ppermute x0 -> x2, waiting for transfers between devices: none -> 126 us  [the longest x1 126 us: per_device_kernels(): lax.ppermute(unit_sums, 'seq', [(at, (at + 2) % 4) for at in range(4)])]
    psum x1, waiting for transfers between devices: 155 us -> 38.4 us  [reduced(): return lax.psum(shard_sum, 'seq').astype(f32)]
    all_to_all x8 -> x0, starting transfers between devices: 38.2 us -> none  [the longest x1 5.85 us: per_device(): lax.all_to_all(values_rep, 'seq', split_axis=1, concat_axis=0, tiled=True)]
    all_to_all x8 -> x0, waiting for transfers between devices: 36.3 us -> none  [the longest x1 10 us: per_device(): lax.all_to_all(attended.reshape(-1, 1, group_heads * HEAD_DIM), 'seq', sp...]
  transfers between devices with their start and end apart: 17 -> 8, of which waited for: 13 -> 5; matrix products, arithmetic and copies ran while one was open for 19% -> 10% of each run, Pallas kernels for 0% -> 11%
where the time goes in v2:
time: 834 us; the launch traced here: 824 us
  waiting for transfers between devices  326 us (39%)
  Pallas kernels  268 us (32%)
  other arithmetic  58 us (7%)
  local copies, waits for them, and re-layouts  55.3 us (7%)
  matrix products  49.4 us (6%)
  blocking collectives  45.7 us (5%)
  between operations  16 us (2%)
    pallas_call x1, Pallas kernels, mlp_ring(): pl.pallas_call(functools.partial(mlp_kernel, size), out_shape=(jax.ShapeD...  175 us
    ppermute x1, waiting for transfers between devices, per_device_kernels(): lax.ppermute(unit_sums, 'seq', [(at, (at + 2) % 4) for at in range(4)])  126 us
    reduce_scatter x1, waiting for transfers between devices, per_device_kernels(): lax.psum_scatter(outs, 'fsdp', scatter_dimension=0, tiled=True).astype(f32)  106 us
    pallas_call x1, Pallas kernels, gather_inputs(): pl.pallas_call(functools.partial(gather_kernel, size), out_shape=tuple((j...  77.4 us
    reduce_scatter x2, waiting for transfers between devices, reduced(): lax.psum_scatter(term.astype(bf16), 'fsdp', scatter_dimension=0, tiled=True)  45.2 us
    unnamed x1, blocking collectives  39.4 us
    psum x1, waiting for transfers between devices, reduced(): return lax.psum(shard_sum, 'seq').astype(f32)  38.4 us
  transfers between devices with their start and end apart: 8, of which 5 were waited for; matrix products, arithmetic and copies ran while one was open for 10% of the time, Pallas kernels for 11%

profile of v2, /device:TPU:2, one launch (start us, length us, event | category | flops | bytes accessed | tf_op | source)
XLA Modules:
  0.0 824.0 jit_solution(4010418536721751272)
XLA Ops:
  13.8 77.4 %gather_inputs.1 = (bf16[4,256,1536]{2,1,0:T(8,128)(2,1)S(1)}, f32[4,256,128]{2,1,0:T(8,128)S(1)}, bf16[8,192,1024]{2,1,0:T(8,128)(2,1)S(1)}, bf16[384,1536]{1,0:T(8,128)(2,1)S(1)}, bf16[8,16,256]{2,1,0:T(8,128)(2,1)S(1)}) custom-call(bf16[256,1536]{1,0:T(8,128)(2,1)S(1)} %bitcast.142, f32[256,128]{1,0:T(8,128)S(1)} %pad_maximum_fusion.6.trig_ref, ...), custom_call_target="tpu_custom_call" | custom-call | tf_op jit(solution)/shard_map/gather_inputs/pallas_call | solution.py:386
  98.3 15.6 %attend_forward.1 = (bf16[1024,1536]{1,0:T(8,128)(2,1)}, bf16[1024,640]{1,0:T(8,128)(2,1)}, bf16[1024,384]{1,0:T(8,128)(2,1)}, f32[1024,128]{1,0:T(8,128)}, bf16[1024,1536]{1,0:T(8,128)(2,1)}) custom-call(bf16[1024,1536]{1,0:T(8,128)(2,1)} %bitcast.147, bf16[1536,1024]{1,0:T(8,128)(2,1)} %bitcast.145, bf16[384,1536]{1,0:T(8,128)(2,1)} %copy-done.7, ...), custom_call_target="tpu_custom_call" | custom-call | flops 4831838208 | bytes 18874368 | tf_op jit(solution)/shard_map/attend_forward/pallas_call | solution.py:491
  119.6 9.6 %all-gather.3.cloned.1.call-done = bf16[1,2048,1536]{2,1,0:T(8,128)(2,1)} async-done(((bf16[1,256,1536]{2,1,0:T(8,128)(2,1)}), bf16[1,2048,1536]{2,1,0:T(8,128)(2,1)}) %all-gather.3.cloned.1.call-update) | async-done | bytes 6291472 | tf_op jit(solution)/shard_map/all_gather | solution.py:970
  129.2 175.5 %mlp_ring.1 = (bf16[2048,1536]{1,0:T(8,128)(2,1)}, f32[256,1536]{1,0:T(8,128)}, bf16[4,256,1536]{2,1,0:T(8,128)(2,1)}, f32[256,1536]{1,0:T(8,128)}, f32[1,1536]{1,0:T(1,128)}, /*index=5*/bf16[3,560,1536]{2,1,0:T(8,128)(2,1)}) custom-call(bf16[256,1536]{1,0:T(8,128)(2,1)} %bitcast.141, bf16[1024,1536]{1,0:T(8,128)(2,1)} %get-tuple-element.85.part_ref, ...), custom_call_target="tpu_custom_call" | custom-call | tf_op jit(solution)/shard_map/mlp_ring/pallas_call | solution.py:876
  304.7 4.6 convolution_convert_fusion.1
  309.3 46.4 %while.15 = (s32[]{:T(128)}, f32[1024,128]{1,0:T(8,128)}, f32[1024,128]{1,0:T(8,128)}, bf16[2,512,3,128]{3,1,0,2:T(8,128)(2,1)}, s32[2]{0:T(128)S(1)}, /*index=5...) while((s32[]{:T(128)}, f32[1024,128]{1,0:T(8,128)}, ...), condition=%wide.region_4.5_spmd.clone, body=%wide.region_2.4_spmd.clone.sunk | while | flops 2038234112 | bytes 94419368 | solution.py:126
  311.8 2.4 fusion.88
  315.3 4.8 fusion.89
  322.1 3.1 fusion.91
  325.2 5.2 fusion.92
  334.9 2.4 fusion.88
  338.4 4.8 fusion.89
  345.2 3.2 fusion.91
  348.4 5.1 fusion.92
  367.7 2.4 fusion.43
  371.0 4.2 convolution_convert_fusion
  375.4 2.7 broadcast_in_dim.57
  379.1 2.5 convolution_dynamic-update-slice_fusion
  383.0 4.8 fusion.55
  387.8 3.5 broadcast_in_dim.55
  394.7 126.0 %collective-permute-done = bf16[3,560,1536]{2,1,0:T(8,128)(2,1)} collective-permute-done((bf16[3,560,1536]{2,1,0:T(8,128)(2,1)}, bf16[3,560,1536]{2,1,0:T(8,128)(2,1)}, u32[]{:S(2)}, u32[]{:S(2)}) %collective-permute-start) | collective-permute-done | bytes 5160992 | tf_op jit(solution)/shard_map/ppermute | solution.py:1059
  520.7 7.8 add_convert_fusion
  534.2 39.4 %all-reduce.6 = (bf16[1536]{0:T(1024)(128)(2,1)S(1)}, bf16[2048]{0:T(1024)(128)(2,1)S(1)}, bf16[1536]{0:T(1024)(128)(2,1)S(1)}) all-reduce(bf16[1536]{0:T(1024)(128)(2,1)S(1)} %get-tuple-element.162, bf16[2048]{0:T(1024)(128)(2,1)S(1)} %convert_element_type.161, ...), channel_id=5, replica_groups=mesh['seq'=4,'fsdp'=8] {'fsdp'}, use_global_device_ids=true, to_apply=%region_8.9.clone | all-reduce | flops 5120 | bytes 20480
  573.8 6.3 all-reduce.7
  581.8 2.7 fusion.39
  584.5 8.8 %broadcast_select_fusion.1 = (bf16[3,560,1536]{2,1,0:T(8,128)(2,1)}, bf16[3,560,1536]{2,1,0:T(8,128)(2,1)}) fusion(bf16[3,560,1536]{2,1,0:T(8,128)(2,1)} %add_convert_fusion, bf16[3,560,1536]{2,1,0:T(8,128)(2,1)} %collective-permute-done.1, pred[]{:T(512)S(6)} %eq.7), kind=kLoop, calls=%fused_computation.42 | loop fusion | flops 5160960 | bytes 20643840 | tf_op jit(solution)/shard_map/jit(_where)/select_n | solution.py:1062
  593.3 12.1 %maximum_convert_fusion = f32[3,1120,1536]{2,1,0:T(8,128)} fusion(bf16[3,560,1536]{2,1,0:T(8,128)(2,1)} %get-tuple-element.200, bf16[3,560,1536]{2,1,0:T(8,128)(2,1)} %get-tuple-element.199), kind=kLoop, calls=%fused_computation.36 | loop fusion | flops 20643840 | bytes 30965760 | tf_op jit(solution)/shard_map/convert_element_type | solution.py:1064
  605.4 45.2 %reduce-scatter.9.cloned.1.call-done = bf16[192,2048]{1,0:T(8,128)(2,1)} async-done(((bf16[1536,2048]{1,0:T(8,128)(2,1)}), bf16[192,2048]{1,0:T(8,128)(2,1)}) %reduce-scatter.9.cloned.1.call-update) | async-done | bytes 786448 | tf_op jit(solution)/shard_map/reduce_scatter | solution.py:1053
  650.6 15.0 %slice_bitcast_fusion = (f32[1120,1536]{1,0:T(8,128)}, f32[1120,1536]{1,0:T(8,128)}, f32[1120,1536]{1,0:T(8,128)}) fusion(f32[3,1120,1536]{2,1,0:T(8,128)} %maximum_convert_fusion), kind=kLoop, calls=%fused_computation.38 | loop fusion | bytes 41287680 | tf_op jit(solution)/shard_map/squeeze | solution.py:1075
  665.6 106.0 %reduce-scatter.5.cloned.1.call-done = bf16[256,1536]{1,0:T(8,128)(2,1)} async-done(((bf16[2048,1536]{1,0:T(8,128)(2,1)}), bf16[256,1536]{1,0:T(8,128)(2,1)}) %reduce-scatter.5.cloned.1.call-update) | async-done | bytes 786448 | tf_op jit(solution)/shard_map/reduce_scatter | solution.py:1003
  773.8 38.4 %all-reduce.11.cloned.1.call-done = (bf16[192,2048]{1,0:T(8,128)(2,1)}, bf16[192,1536]{1,0:T(8,128)(2,1)}) async-done(((bf16[192,2048]{1,0:T(8,128)(2,1)}, bf16[192,1536]{1,0:T(8,128)(2,1)}), (bf16[192,2048]{1,0:T(8,128)(2,1)}, bf16[192,1536]{1,0:T(8,128)(2,1)})) %all-reduce.11.cloned.1.call-update) | async-done | bytes 1376272 | tf_op jit(solution)/shard_map/psum | solution.py:1056
  812.3 2.5 convert_element_type.159
  (169 shorter events, 59.8 us)
Async XLA Ops:
  7.2 6.6 copy-start
  7.2 122.0 %all-gather.3.cloned.1.call-start = ((), (), s32[]{:S(2)}) async-start(), calls=%async_computation.8 | async-start | bytes 7077888 | tf_op jit(solution)/shard_map/all_gather | solution.py:970
  7.9 524.4 %reduce-scatter.7.cloned.1.call-start = ((), (), s32[]{:S(2)}) async-start(), calls=%async_computation.5 | async-start | bytes 3932160 | tf_op jit(solution)/shard_map/reduce_scatter | solution.py:1029
  113.9 4.5 copy-start.3
  304.7 4.6 copy-start.11
  314.2 5.9 copy-start.8
  315.3 4.8 copy-start.9
  322.0 3.1 copy-start.10
  322.0 3.1 copy-start.23
  325.2 5.2 copy-start.13
  337.3 5.9 copy-start.8
  338.4 4.8 copy-start.9
  345.2 3.3 copy-start.10
  345.2 3.3 copy-start.23
  348.4 5.1 copy-start.13
  355.6 3.1 copy-start.12
  355.6 3.1 copy-start.18
  365.5 5.5 copy-start.5
  367.7 3.3 copy-start.21
  375.3 3.3 copy-start.27
  375.3 230.1 %reduce-scatter.11.cloned.1.call-start = ((), (), s32[]{:S(2)}) async-start(), calls=%async_computation.7 | async-start | bytes 5308416 | tf_op jit(solution)/shard_map/reduce_scatter | solution.py:1053
  375.4 3.7 copy-start.29
  381.6 269.0 %reduce-scatter.9.cloned.1.call-start = ((), (), s32[]{:S(2)}) async-start(), calls=%async_computation.6 | async-start | bytes 7077888 | tf_op jit(solution)/shard_map/reduce_scatter | solution.py:1053
  394.0 377.7 %reduce-scatter.5.cloned.1.call-start = ((), (), s32[]{:S(2)}) async-start(), calls=%async_computation.4 | async-start | bytes 7077888 | tf_op jit(solution)/shard_map/reduce_scatter | solution.py:1003
  394.0 126.7 %collective-permute-start = (bf16[3,560,1536]{2,1,0:T(8,128)(2,1)}, bf16[3,560,1536]{2,1,0:T(8,128)(2,1)}, u32[]{:S(2)}, u32[]{:S(2)}) collective-permute-start(bf16[3,560,1536]{2,1,0:T(8,128)(2,1)} %get-tuple-element.98), channel_id=1, source_target_pairs={{0,16},{8,24},{16,0},{24,8},{1,17},{9,25},{17,1},{25,9},{2,18},{10... | collective-permute-start | bytes 15482888 | tf_op jit(solution)/shard_map/ppermute | solution.py:1059
  394.6 134.0 %copy-start.28 = (u32[32]{0:T(128)S(1)}, u32[32]{0:T(128)}, u32[]{:S(2)}) copy-start(u32[32]{0:T(128)} %constant.104) | copy-start | bytes 388
  394.7 135.9 %copy-start.1 = (bf16[1,256,1536]{2,1,0:T(8,128)(2,1)S(1)}, bf16[1,256,1536]{2,1,0:T(8,128)(2,1)}, u32[]{:S(2)}) copy-start(bf16[1,256,1536]{2,1,0:T(8,128)(2,1)} %param.13) | copy-start | bytes 2359300
  394.7 137.6 %copy-start.26 = (f32[1,1536]{1,0:T(1,128)S(1)}, f32[1,1536]{1,0:T(1,128)}, u32[]{:S(2)}) copy-start(f32[1,1536]{1,0:T(1,128)} %get-tuple-element.97) | copy-start | bytes 18436
  394.7 417.6 %all-reduce.11.cloned.1.call-start = ((), (), s32[]{:S(2)}) async-start(), calls=%async_computation.9 | async-start | bytes 2752512 | tf_op jit(solution)/shard_map/psum | solution.py:1056
  528.6 53.2 %copy-start.20 = (f32[256,1536]{1,0:T(8,128)S(1)}, f32[256,1536]{1,0:T(8,128)}, u32[]{:S(2)}) copy-start(f32[256,1536]{1,0:T(8,128)} %get-tuple-element.88) | copy-start | bytes 4718596
  528.6 55.9 %collective-permute-start.1 = (bf16[3,560,1536]{2,1,0:T(8,128)(2,1)}, bf16[3,560,1536]{2,1,0:T(8,128)(2,1)}, u32[]{:S(2)}, u32[]{:S(2)}) collective-permute-start(bf16[3,560,1536]{2,1,0:T(8,128)(2,1)} %add_convert_fusion), channel_id=1, source_target_pairs={{0,8},{8,0},{16,24},{24,16},{1,9},{9,1},{17,25},{25,17},{2,10},{10... | collective-permute-start | bytes 15482888 | tf_op jit(solution)/shard_map/ppermute | solution.py:1061
  650.6 121.0 %copy-start.19 = (f32[256,1536]{1,0:T(8,128)S(1)}, f32[256,1536]{1,0:T(8,128)}, u32[]{:S(2)}) copy-start(f32[256,1536]{1,0:T(8,128)} %get-tuple-element.86) | copy-start | bytes 4718596
  (13 other events, 17.6 us)
Sparse Core Ops, SparseCore 0:
  10.2 118.9 all-gather.2
  375.4 48.5 reduce-scatter.6
  428.1 99.6 reduce-scatter.10
  532.2 118.3 reduce-scatter.8
  654.4 117.1 reduce-scatter.4
  774.1 38.0 all-reduce.10

commit v3 on v2

--- a/solution.py
+++ b/solution.py
@@ -840,12 +840,22 @@
                 grads[at, span, :] + weights[at, span, :].astype(jnp.float32)
             ).astype(jnp.bfloat16)
 
+        done = weights.at[at, pl.ds(kept, share)]
         stores.append(
-            pltpu.make_async_copy(
-                weights.at[at, pl.ds(kept, share)], sums_ref.at[at], load_sems.at[at]
+            pltpu.make_async_copy(done, sums_ref.at[at, pl.ds(kept, share)], load_sems.at[at])
+        )
+        swaps.append(
+            pltpu.make_async_remote_copy(
+                src_ref=done,
+                dst_ref=sums_ref.at[at, pl.ds(kept, share)],
+                send_sem=swap_send.at[3 + at],
+                recv_sem=swap_recv.at[3 + at],
+                device_id={"seq": core},
+                device_id_type=MESH,
             )
         )
         stores[-1].start()
+        swaps[-1].start()
     to_far.wait_recv()
     passed_on.start()
     for side in range(2):
@@ -860,6 +870,8 @@
         copy.wait_send()
     to_core.wait_recv()
     passed_on.wait_recv()
+    for copy in swaps[3:]:
+        copy.wait_recv()
     for store in stores + [keep, resid_store]:
         store.wait()
 
@@ -881,7 +893,7 @@
             jax.ShapeDtypeStruct((groups, tokens, width), bf16),
             jax.ShapeDtypeStruct((tokens, width), f32),
             jax.ShapeDtypeStruct((1, width), f32),
-            jax.ShapeDtypeStruct((3, units // 2, width), bf16),
+            jax.ShapeDtypeStruct((3, units, width), bf16),
         ),
         in_specs=[anywhere, anywhere, inside, anywhere, anywhere, anywhere, anywhere],
         out_specs=(anywhere, anywhere, anywhere, inside, inside, anywhere),
@@ -909,8 +921,8 @@
             dma((2, size)),
             dma((6,)),
             dma((6,)),
-            dma((3,)),
-            dma((3,)),
+            dma((6,)),
+            dma((6,)),
             pltpu.SemaphoreType.REGULAR,
         ],
         compiler_params=pltpu.CompilerParams(
@@ -920,11 +932,495 @@
     )(hidden, part, gain, cots, gate_weight, up_weight, down_weight)
 
 
+def attend_backward_kernel(
+    size,
+    block,
+    grads_ref,
+    heads_ref,
+    attended_ref,
+    log_ref,
+    proj_ref,
+    weight_ref,
+    normed_ref,
+    trig_ref,
+    hidden_ref,
+    resid_grad_ref,
+    gain_ref,
+    gain_grad_ref,
+    resid_ref,
+    outs_ref,
+    units_ref,
+    grad_in_ref,
+    hidden_out_ref,
+    small_ref,
+    shards_ref,
+    far_units_ref,
+    grad_heads,
+    grad_mixed,
+    grad_keys,
+    grad_values,
+    grad_normed,
+    term_qkv,
+    term_out,
+    out_columns,
+    qkv_in,
+    out_in,
+    qkv_sum,
+    out_sum,
+    shard,
+    shard_all,
+    out_own,
+    out_recv,
+    out_send,
+    resid,
+    seq_in,
+    far_sum,
+    small_in,
+    load_sems,
+    own_sems,
+    out_sems,
+    term_sems,
+    column_sems,
+    seq_sems,
+    shard_sems,
+    small_sems,
+    unit_sems,
+    pass_sems,
+):
+    length, width = grads_ref.shape
+    tokens = hidden_ref.shape[0]
+    used = heads_ref.shape[1]
+    own = attended_ref.shape[1]
+    count = own // HEAD_DIM
+    scale = HEAD_DIM**-0.5
+    half = tokens // 2
+    depth = width // size
+    term_half = depth // 2
+    units = units_ref.shape[1]
+    f32, bf16 = jnp.float32, jnp.bfloat16
+    me = lax.axis_index("fsdp")
+    seq = lax.axis_index("seq")
+    place = ring_place(me, size)
+    right = ring_member((place + 1) % size, size)
+    left = ring_member((place + size - 1) % size, size)
+    core, far, diagonal = seq_partners(seq)
+    rounds = size.bit_length() - 1
+    mirrors = [me + (1 - 2 * ((me // 2**at) % 2)) * 2**at for at in range(rounds)]
+    ring = ({"fsdp": right}, {"fsdp": left})
+
+    def owner_of(step, side):
+        return ring_member((place + size - step if side == 0 else place + step) % size, size)
+
+    def remote(source, target, sems, at, device):
+        return pltpu.make_async_remote_copy(
+            src_ref=source,
+            dst_ref=target,
+            send_sem=sems.at[(0,) + at],
+            recv_sem=sems.at[(1,) + at],
+            device_id=device,
+            device_id_type=MESH,
+        )
+
+    greet(
+        ring
+        + ({"seq": core}, {"seq": far}, {"seq": diagonal})
+        + tuple({"fsdp": mirror} for mirror in mirrors)
+    )
+
+    def own_load(step, side):
+        at = pl.multiple_of(owner_of(step, side) * tokens + side * half, half)
+        return pltpu.make_async_copy(
+            outs_ref.at[pl.ds(at, half)],
+            out_own.at[step % 2, pl.ds(side * half, half)],
+            own_sems.at[step % 2, side],
+        )
+
+    def out_copy(step, side):
+        span = pl.ds(side * half, half)
+        return remote(
+            out_send.at[step % 2, span], out_recv.at[step, span], out_sems, (side, step), ring[side]
+        )
+
+    def out_step(step):
+        for side in range(2):
+            own_load(step, side).wait()
+            if step < size - 1:
+                own_load(step + 1, side).start()
+            if step >= 3:
+                out_copy(step - 2, side).wait_send()
+            if step >= 2:
+                out_copy(step - 1, side).wait_recv()
+        total = out_own[step % 2].astype(f32)
+        if step >= 2:
+            total += out_recv[step - 1].astype(f32)
+        out_send[step % 2] = total.astype(bf16)
+        for side in range(2):
+            out_copy(step, side).start()
+
+    resid_load = pltpu.make_async_copy(resid_ref, resid, load_sems.at[0])
+
+    def out_finish():
+        step = size
+        for side in range(2):
+            out_copy(step - 2, side).wait_send()
+            out_copy(step - 1, side).wait_send()
+            out_copy(step - 1, side).wait_recv()
+        mine = pltpu.make_async_copy(
+            outs_ref.at[pl.ds(pl.multiple_of(me * tokens, tokens), tokens)],
+            out_own.at[0],
+            load_sems.at[1],
+        )
+        mine.start()
+        mine.wait()
+        resid_load.wait()
+        hidden_out_ref[...] = (
+            resid[...] + out_own[0].astype(f32) + out_recv[size - 1].astype(f32)
+        ).astype(bf16)
+
+    share = units // 2
+    piece = share // 5
+    kept = (seq % 2) * share
+
+    def unit_slice(ref, at):
+        start = pl.multiple_of(kept + (at % 5) * piece, 16)
+        return ref.at[at // 5, pl.ds(start, piece)]
+
+    def unit_copy(at):
+        return remote(
+            unit_slice(units_ref, at), unit_slice(far_units_ref, at), unit_sems, (at,), {"seq": far}
+        )
+
+    def unit_pass(at):
+        part = unit_slice(far_units_ref, at)
+        return remote(part, part, pass_sems, (at,), {"seq": core})
+
+    chunks = 15
+    lag = 4
+
+    def pump(at):
+        if at < chunks:
+            unit_copy(at).start()
+        if at % 2 == 0 and at // 2 + 1 < size:
+            out_step(at // 2 + 1)
+        if lag <= at < chunks + lag:
+            unit_copy(at - lag).wait_recv()
+            unit_pass(at - lag).start()
+
+    resid_load.start()
+    for side in range(2):
+        own_load(1, side).start()
+    pump(0)
+
+    for start in range(0, length, block):
+        span = slice(start, start + block)
+        grad_heads[span, :] = matmul(grads_ref[span, :], proj_ref[...], NT).astype(bf16)
+
+    def out_term(span):
+        term_out[:, span] = matmul(attended_ref[...], grads_ref[:, span], TN).astype(bf16)
+
+    for_blocks(width, 256, out_term)
+
+    def column_copy(at, target):
+        slot = pl.multiple_of(seq * own, 16)
+        return remote(
+            term_out.at[:, pl.ds(pl.multiple_of(target * own, 128), own)],
+            out_columns.at[pl.ds(slot, own)],
+            column_sems,
+            (at,),
+            {"seq": target},
+        )
+
+    columns = [column_copy(at, target) for at, target in enumerate((core, far, diagonal))]
+    for copy in columns:
+        copy.start()
+    mine = pl.multiple_of(seq * own, 128)
+    out_columns[pl.ds(mine, own), :] = term_out[:, pl.ds(mine, own)]
+    pump(1)
+    grad_keys[...] = jnp.zeros_like(grad_keys)
+    grad_values[...] = jnp.zeros_like(grad_values)
+    lane = lax.broadcasted_iota(jnp.int32, (block, HEAD_DIM), 1)
+    keys = slice(own, own + HEAD_DIM)
+    values = slice(own + HEAD_DIM, used)
+    for turn, start in enumerate(range(0, length, block)):
+        span = slice(start, start + block)
+        seen = slice(0, start + block)
+        cosine, sine = turn_tables(trig_ref[span, :])
+
+        @pl.loop(0, count)
+        def _(at):
+            head = pl.ds(pl.multiple_of(at * HEAD_DIM, HEAD_DIM), HEAD_DIM)
+            query = heads_ref[span, head]
+            grad = grad_heads[span, head]
+            logs = jnp.sum(jnp.where(lane == at, log_ref[span, :], 0.0), axis=-1, keepdims=True)
+            scores = causal(matmul(query, heads_ref[seen, keys], NT) * scale, start)
+            probability = jnp.exp(scores - logs)
+            grad_probs = matmul(grad, heads_ref[seen, values], NT)
+            delta = jnp.sum(probability * grad_probs, axis=-1, keepdims=True)
+            grad_scores = (probability * (grad_probs - delta)).astype(bf16)
+            grad_query = matmul(grad_scores, heads_ref[seen, keys], NN) * scale
+            grad_query = grad_query.astype(bf16).astype(f32)
+            grad_mixed[span, head] = (
+                grad_query * cosine + pltpu.roll(grad_query * sine, HEAD_DIM // 2, 1)
+            ).astype(bf16)
+            grad_keys[seen, :] += matmul(grad_scores, query, TN) * scale
+            grad_values[seen, :] += matmul(probability.astype(bf16), grad, TN)
+
+        pump(2 + turn)
+
+    for start in range(0, length, block):
+        span = slice(start, start + block)
+        cosine, sine = turn_tables(trig_ref[span, :])
+        part = grad_keys[span, :].astype(bf16).astype(f32)
+        grad_mixed[span, keys] = (
+            part * cosine + pltpu.roll(part * sine, HEAD_DIM // 2, 1)
+        ).astype(bf16)
+        grad_mixed[span, values] = grad_values[span, :].astype(bf16)
+
+    def normed_part(span):
+        grad_normed[:, span] = matmul(grad_mixed[...], weight_ref[span, :used], NT).astype(bf16)
+
+    for_blocks(width, 256, normed_part)
+
+    def block_rows(at):
+        return grad_normed.at[pl.ds(pl.multiple_of(at * tokens, tokens), tokens)]
+
+    to_core = [
+        remote(block_rows(diagonal), seq_in.at[0], seq_sems, (0,), {"seq": core}),
+        remote(block_rows(core), seq_in.at[1], seq_sems, (1,), {"seq": core}),
+    ]
+    to_far = remote(far_sum, seq_in.at[2], seq_sems, (2,), {"seq": far})
+    for copy in to_core:
+        copy.start()
+
+    def qkv_term(span):
+        term_qkv[span, :] = matmul(normed_ref[:, span], grad_mixed[...], TN).astype(bf16)
+
+    for_blocks(width, 256, qkv_term)
+    to_core[0].wait_recv()
+    far_sum[...] = (block_rows(far)[...].astype(f32) + seq_in[0].astype(f32)).astype(bf16)
+    to_far.start()
+    small_in[0] = jnp.zeros((8, width), f32)
+    small_in[0, 1:2, :] = gain_grad_ref[...]
+    bias = jnp.sum(grad_mixed[...].astype(f32), axis=0, keepdims=True)
+    small_in[0, 2:3, pl.ds(mine, own)] = bias[:, :own]
+    kv_lane = pl.multiple_of((seq // 2) * HEAD_DIM, HEAD_DIM)
+    small_in[0, 3:4, pl.ds(kv_lane, HEAD_DIM)] = bias[:, keys]
+    small_in[0, 3:4, pl.ds(kv_lane + KV_HEADS * HEAD_DIM, HEAD_DIM)] = bias[:, values]
+    pump(6)
+
+    def term_rows(step, side):
+        return pl.ds(
+            pl.multiple_of(owner_of(step, side) * depth + side * term_half, 16), term_half
+        )
+
+    def term_copy(which, step, side):
+        held, landed = ((qkv_sum, qkv_in), (out_sum, out_in))[which]
+        span = pl.ds(side * term_half, term_half)
+        return remote(
+            held.at[step % 2, span], landed.at[step, span], term_sems, (which, side, step), ring[side]
+        )
+
+    def term_step(which, step):
+        source, held, landed = ((term_qkv, qkv_sum, qkv_in), (out_columns, out_sum, out_in))[which]
+        for side in range(2):
+            if step >= 3:
+                term_copy(which, step - 2, side).wait_send()
+            total = source[term_rows(step, side), :].astype(f32)
+            span = pl.ds(side * term_half, term_half)
+            if step >= 2:
+                term_copy(which, step - 1, side).wait_recv()
+                total += landed[step - 1, span, :].astype(f32)
+            held[step % 2, span, :] = total.astype(bf16)
+            term_copy(which, step, side).start()
+
+    def small_copy(at):
+        device = ({"seq": core}, {"seq": far})[at] if at < 2 else {"fsdp": mirrors[at - 2]}
+        return remote(small_in.at[2 * at], small_in.at[2 * at + 1], small_sems, (at,), device)
+
+    def small_step(at):
+        small_copy(at).wait_recv()
+        small_in[2 * at + 2] = small_in[2 * at] + small_in[2 * at + 1]
+
+    term_step(0, 1)
+    for copy in columns:
+        copy.wait_recv()
+    term_step(1, 1)
+    term_step(0, 2)
+    term_step(1, 2)
+    to_core[1].wait_recv()
+    to_far.wait_recv()
+    rows = hidden_ref[...].astype(f32)
+    inverse = lax.rsqrt(jnp.mean(rows * rows, axis=-1, keepdims=True) + norm_eps)
+    unit_rows = rows * inverse
+    grad_rows = (
+        block_rows(seq)[...].astype(f32) + seq_in[1].astype(f32) + seq_in[2].astype(f32)
+    )
+    small_in[0, 0:1, :] = jnp.sum(grad_rows * unit_rows, axis=0, keepdims=True)
+    small_copy(0).start()
+    grad_unit = grad_rows * gain_ref[...]
+    grad_in_ref[...] = resid_grad_ref[...] + inverse * (
+        grad_unit - unit_rows * jnp.mean(grad_unit * unit_rows, axis=-1, keepdims=True)
+    )
+    pump(7)
+    total_rounds = rounds + 2
+    done = 0
+    for step in range(3, size):
+        for which in range(2):
+            term_step(which, step)
+        if done < total_rounds:
+            small_step(done)
+            done += 1
+            if done < total_rounds:
+                small_copy(done).start()
+        pump(5 + step)
+    while done < total_rounds:
+        small_step(done)
+        done += 1
+        if done < total_rounds:
+            small_copy(done).start()
+    small_ref[...] = small_in[2 * total_rounds]
+    for which in range(2):
+        source, landed = ((term_qkv, qkv_in), (out_columns, out_in))[which]
+        lanes = slice(0, used) if which == 0 else slice(used, used + own)
+        for side in range(2):
+            span = pl.ds(side * term_half, term_half)
+            term_copy(which, size - 2, side).wait_send()
+            term_copy(which, size - 1, side).wait_send()
+            term_copy(which, size - 1, side).wait_recv()
+            shard[span, lanes] = (
+                source[pl.ds(pl.multiple_of(me * depth + side * term_half, 16), term_half), :].astype(f32)
+                + landed[size - 1, span, :].astype(f32)
+            ).astype(bf16)
+    shard_far = remote(shard, shard_all.at[seq], shard_sems, (0,), {"seq": far})
+    shard_core = remote(shard, shard_all.at[seq], shard_sems, (1,), {"seq": core})
+    shard_pass = remote(shard_all.at[far], shard_all.at[far], shard_sems, (2,), {"seq": core})
+    shard_far.start()
+    shard_core.start()
+    shard_all[seq] = shard[...]
+    for at in range(5 + size, chunks):
+        pump(at)
+    shard_far.wait_recv()
+    shard_pass.start()
+    out_finish()
+    for at in range(max(chunks, 5 + size), chunks + lag):
+        pump(at)
+    shard_core.wait_recv()
+    shard_pass.wait_recv()
+    store = pltpu.make_async_copy(shard_all, shards_ref, load_sems.at[1])
+    store.start()
+    for at in range(chunks):
+        unit_pass(at).wait_recv()
+        unit_copy(at).wait_send()
+        unit_pass(at).wait_send()
+    for at in range(total_rounds):
+        small_copy(at).wait_send()
+    for copy in columns + to_core + [to_far, shard_far, shard_core, shard_pass]:
+        copy.wait_send()
+    store.wait()
+
+
+def attend_group_backward(
+    grads,
+    heads,
+    attended,
+    logs,
+    proj,
+    weight,
+    normed,
+    trig,
+    hidden,
+    resid_grad,
+    gain,
+    gain_grad,
+    resid,
+    outs,
+    units,
+):
+    size = lax.axis_size("fsdp")
+    groups = lax.axis_size("seq")
+    length, width = grads.shape
+    tokens = hidden.shape[0]
+    used = heads.shape[1]
+    own = attended.shape[1]
+    depth = width // size
+    rounds = size.bit_length() + 1
+    bf16, f32 = jnp.bfloat16, jnp.float32
+    anywhere = pl.BlockSpec(memory_space=pl.ANY)
+    inside = pl.BlockSpec(memory_space=pltpu.VMEM)
+    dma = pltpu.SemaphoreType.DMA
+    vmem = pltpu.VMEM
+    return pl.pallas_call(
+        functools.partial(attend_backward_kernel, size, 256),
+        out_shape=(
+            jax.ShapeDtypeStruct((tokens, width), f32),
+            jax.ShapeDtypeStruct((tokens, width), bf16),
+            jax.ShapeDtypeStruct((8, width), f32),
+            jax.ShapeDtypeStruct((groups, depth, used + own), bf16),
+            jax.ShapeDtypeStruct(units.shape, bf16),
+        ),
+        in_specs=[inside] * 12 + [anywhere] * 3,
+        out_specs=(inside, inside, inside, anywhere, anywhere),
+        scratch_shapes=[
+            vmem((length, own), bf16),
+            vmem((length, used), bf16),
+            vmem((length, HEAD_DIM), f32),
+            vmem((length, HEAD_DIM), f32),
+            vmem((length, width), bf16),
+            vmem((width, used), bf16),
+            vmem((own, width), bf16),
+            vmem((width, own), bf16),
+            vmem((size, depth, used), bf16),
+            vmem((size, depth, own), bf16),
+            vmem((2, depth, used), bf16),
+            vmem((2, depth, own), bf16),
+            vmem((depth, used + own), bf16),
+            vmem((groups, depth, used + own), bf16),
+            vmem((2, tokens, width), bf16),
+            vmem((size, tokens, width), bf16),
+            vmem((2, tokens, width), bf16),
+            vmem((tokens, width), f32),
+            vmem((3, tokens, width), bf16),
+            vmem((tokens, width), bf16),
+            vmem((2 * rounds + 1, 8, width), f32),
+            dma((2,)),
+            dma((2, 2)),
+            dma((2, 2, size)),
+            dma((2, 2, 2, size)),
+            dma((2, 3)),
+            dma((2, 3)),
+            dma((2, 3)),
+            dma((2, rounds)),
+            dma((2, 15)),
+            dma((2, 15)),
+        ],
+        compiler_params=pltpu.CompilerParams(
+            collective_id=2, has_side_effects=True, vmem_limit_bytes=VMEM_BYTES
+        ),
+        name="attend_backward",
+    )(
+        grads,
+        heads,
+        attended,
+        logs,
+        proj,
+        weight,
+        normed,
+        trig,
+        hidden,
+        resid_grad,
+        gain,
+        gain_grad,
+        resid,
+        outs,
+        units,
+    )
+
+
 def kernels_fit(hidden_in, positions, attn_gain, qkv_weight, qkv_bias, out_weight, *rest):
     size, groups = lax.axis_size("fsdp"), lax.axis_size("seq")
     _, tokens, width = hidden_in.shape
     units = rest[1].shape[0]
-    if groups != 4 or size % 4 or tokens % 256 or units % 32 or width % 512:
+    if groups != 4 or size % 4 or size & (size - 1) or tokens % 256 or units % 160 or width % 512:
         return False
     if (width // size) % 32 or qkv_bias.shape[0] > 256 or KV_HEADS != 2:
         return False
@@ -1000,80 +1496,44 @@
     outs, residual, proj_grads, grad_residual, term_gain_two, unit_sums = mlp_ring(
         hidden_in[0], part, gain_two, all_cots, gate_weight, up_weight, down_weight
     )
-    mlp_out = lax.psum_scatter(outs, "fsdp", scatter_dimension=0, tiled=True).astype(f32)
-    hidden_out = (residual + mlp_out).astype(bf16)
-    proj_grads = proj_grads.reshape(length, width)
-
-    count = own // HEAD_DIM
-    grad_heads = jnp.einsum("td,ed->te", proj_grads, proj, preferred_element_type=f32).astype(bf16)
-    term_out = jnp.einsum("te,td->ed", attended, proj_grads, preferred_element_type=f32)
-    grad_query, grad_keys, grad_values = attend_backward(
-        heads[:, :own].reshape(length, count, HEAD_DIM),
-        heads[:, own : own + HEAD_DIM],
-        heads[:, own + HEAD_DIM :],
-        logs[:, :count].reshape(2, length // 2, count).transpose(0, 2, 1),
-        grad_heads.reshape(length, count, HEAD_DIM),
-    )
-    cosine_all = jnp.concatenate([trig_all[:, :half_dim]] * 2, axis=1)
-    sine_all = jnp.concatenate([trig_all[:, half_dim:]] * 2, axis=1)
-    grad_query = unrotate(grad_query.astype(bf16).astype(f32), cosine_all, sine_all)
-    grad_keys = unrotate(grad_keys.astype(bf16).astype(f32)[:, None], cosine_all, sine_all)[:, 0]
-    grad_mixed = jnp.concatenate(
-        [grad_query.reshape(length, own), grad_keys, grad_values.astype(bf16).astype(f32)], axis=1
-    ).astype(bf16)
-    term_qkv = jnp.einsum("td,tc->dc", normed_one, grad_mixed, preferred_element_type=f32)
-    term_bias = jnp.sum(grad_mixed.astype(f32), axis=0)
-    grad_normed = jnp.einsum(
-        "tc,dc->td", grad_mixed, weight[:, :used], preferred_element_type=f32
-    )
-    grad_normed = lax.psum_scatter(grad_normed.astype(bf16), "seq", scatter_dimension=0, tiled=True)
-    unit_one, inverse_one, _ = norm_forward(hidden_in[0].astype(f32), gain_one)
-    grad_norm_one, term_gain_one = norm_backward(
-        grad_normed.astype(f32), unit_one, inverse_one, gain_one
-    )
-    grad_rows = grad_residual + grad_norm_one
-
-    width_query = HEADS * HEAD_DIM
-
-    def spread(term):
-        full = jnp.zeros(term.shape[:-1] + (width_query + 2 * KV_HEADS * HEAD_DIM,), f32)
-        kv_head = seq // 2
-        full = lax.dynamic_update_slice_in_dim(full, term[..., :own], seq * own, term.ndim - 1)
-        full = lax.dynamic_update_slice_in_dim(
-            full, term[..., own : own + HEAD_DIM], width_query + kv_head * HEAD_DIM, term.ndim - 1
-        )
-        return lax.dynamic_update_slice_in_dim(
-            full,
-            term[..., own + HEAD_DIM :],
-            width_query + (KV_HEADS + kv_head) * HEAD_DIM,
-            term.ndim - 1,
-        )
-
-    def reduced(term):
-        shard_sum = lax.psum_scatter(
-            term.astype(bf16), "fsdp", scatter_dimension=0, tiled=True
-        )
-        return lax.psum(shard_sum, "seq").astype(f32)
-
-    full_out = lax.dynamic_update_slice_in_dim(jnp.zeros((width, width), f32), term_out, seq * own, 0)
-    far_sums = lax.ppermute(unit_sums, "seq", [(at, (at + 2) % 4) for at in range(4)])
-    totals = (unit_sums.astype(f32) + far_sums.astype(f32)).astype(bf16)
-    others = lax.ppermute(totals, "seq", [(at, at + 1 - 2 * (at % 2)) for at in range(4)])
-    first = jnp.where(seq % 2 == 0, totals, others)
-    second = jnp.where(seq % 2 == 0, others, totals)
-    units_grads = jnp.concatenate([first, second], axis=1).astype(f32)
+    grad_rows, hidden_out, smalls, shards, far_sums = attend_group_backward(
+        proj_grads.reshape(length, width),
+        heads,
+        attended,
+        logs,
+        proj,
+        weight,
+        normed_one,
+        trig_all,
+        hidden_in[0],
+        grad_residual,
+        gain_one,
+        term_gain_two,
+        residual,
+        outs,
+        unit_sums,
+    )
+    shards = shards.astype(f32)
+    keys = shards[:, :, own : own + HEAD_DIM]
+    values = shards[:, :, own + HEAD_DIM : used]
+    grad_qkv = jnp.concatenate(
+        [shards[at, :, :own] for at in range(groups)]
+        + [part[2 * at] + part[2 * at + 1] for part in (keys, values) for at in range(KV_HEADS)],
+        axis=1,
+    )
+    grad_out = jnp.concatenate([shards[at, :, used:] for at in range(groups)], axis=1)
+    me = lax.axis_index("fsdp")
+    bias_sums = jnp.concatenate([smalls[2], smalls[3, : 2 * KV_HEADS * HEAD_DIM]])
+    bias_shard = qkv_bias.shape[0]
     return (
         hidden_out[None],
         grad_rows[None],
-        reduced(term_gain_one),
-        reduced(spread(term_qkv)),
-        reduced(spread(term_bias)),
-        reduced(full_out),
-        reduced(term_gain_two[0]),
-        units_grads[0],
-        units_grads[1],
-        units_grads[2],
-    )
+        lax.dynamic_slice_in_dim(smalls[0], me * shard, shard),
+        grad_qkv,
+        lax.dynamic_slice_in_dim(bias_sums, me * bias_shard, bias_shard),
+        grad_out,
+        lax.dynamic_slice_in_dim(smalls[1], me * shard, shard),
+    ) + tuple(unit_sums[at].astype(f32) + far_sums[at].astype(f32) for at in range(3))
 
 
 def per_device_gathered(

time: 834 us -> 502 us (0.60)
  waiting for transfers between devices: 326 us -> 16.6 us
  Pallas kernels: 268 us -> 432 us
  matrix products: 49.4 us -> 0 us
  blocking collectives: 45.7 us -> 0 us
  local copies, waits for them, and re-layouts: 55.3 us -> 15.5 us
  other arithmetic: 58 us -> 21.2 us
    pallas_call x0 -> x1, Pallas kernels: none -> 163 us  [attend_group_backward(): pl.pallas_call(functools.partial(attend_backward_kernel, size, 256), out_...]
    reduce_scatter x4 -> x0, waiting for transfers between devices: 151 us -> none  [the longest x1 106 us: per_device_kernels(): lax.psum_scatter(outs, 'fsdp', scatter_dimension=0, tiled=True).astype(f32)]
    ppermute x2 -> x0, waiting for transfers between devices: 126 us -> none  [the longest x1 126 us: per_device_kernels(): lax.ppermute(unit_sums, 'seq', [(at, (at + 2) % 4) for at in range(4)])]
    dot_general x14 -> x0, matrix products: 49.4 us -> none  [the longest x2 10.3 us: one_block(): jnp.einsum('hbl,bhd->ld', probability.astype(jnp.bfloat16), grad_block, p...]
    unnamed x1 -> x0, blocking collectives: 39.4 us -> none
    psum x1 -> x0, waiting for transfers between devices: 38.4 us -> none  [reduced(): return lax.psum(shard_sum, 'seq').astype(f32)]
    convert_element_type x11 -> x1, other arithmetic: 30.1 us -> 1.79 us  [per_device_kernels(): shards = shards.astype(f32)]
    squeeze x1, local copies, waits for them, and re-layouts: 15 us -> 0.12 us  [per_device_kernels(): shards[at, :, used:]]
  transfers between devices with their start and end apart: 8 -> 1, of which waited for: 5 -> 1; matrix products, arithmetic and copies ran while one was open for 10% -> 2% of each run, Pallas kernels for 11% -> 19%
where the time goes in v3:
time: 502 us; the launch traced here: 499 us
  Pallas kernels  432 us (86%)
  other arithmetic  21.2 us (4%)
  waiting for transfers between devices  16.6 us (3%)
  local copies, waits for them, and re-layouts  15.5 us (3%)
  between operations  14.3 us (3%)
    pallas_call x1, Pallas kernels, mlp_ring(): pl.pallas_call(functools.partial(mlp_kernel, size), out_shape=(jax.ShapeD...  176 us
    pallas_call x1, Pallas kernels, attend_group_backward(): pl.pallas_call(functools.partial(attend_backward_kernel, size, 256), out_...  163 us
    pallas_call x1, Pallas kernels, gather_inputs(): pl.pallas_call(functools.partial(gather_kernel, size), out_shape=tuple((j...  77.1 us
    all_gather x1, waiting for transfers between devices, per_device_kernels(): all_cots = lax.all_gather(cotangent[0], 'fsdp', axis=0, tiled=True)  15.9 us
    pallas_call x1, Pallas kernels, attend_group(): pl.pallas_call(functools.partial(attend_forward_kernel, 256), out_shape=(...  15.6 us
    add x1, other arithmetic, per_device_kernels(): unit_sums[at].astype(f32) + far_sums[at].astype(f32)  15 us
  transfers between devices with their start and end apart: 1, of which 1 were waited for; matrix products, arithmetic and copies ran while one was open for 2% of the time, Pallas kernels for 19%

profile of v3, /device:TPU:2, one launch (start us, length us, event | category | flops | bytes accessed | tf_op | source)
XLA Modules:
  0.0 499.3 jit_solution(10610484305633125037)
XLA Ops:
  7.2 0.7 all-gather.3.cloned.1.call-update
  7.9 0.7 convert_element_type.55
  8.6 0.7 pad.11
  9.3 0.7 pad.12
  10.0 0.7 stack.14
  10.7 0.8 constant_dynamic-slice_fusion.7
  11.6 0.9 maximum_cosine_fusion
  12.5 0.1 pad_maximum_fusion.3.trig_ref
  12.6 1.0 constant_dynamic-slice_fusion.5
  13.7 77.1 %gather_inputs.1 = (bf16[4,256,1536]{2,1,0:T(8,128)(2,1)S(1)}, f32[4,256,128]{2,1,0:T(8,128)S(1)}, bf16[8,192,1024]{2,1,0:T(8,128)(2,1)S(1)}, bf16[384,1536]{1,0:T(8,128)(2,1)S(1)}, bf16[8,16,256]{2,1,0:T(8,128)(2,1)S(1)}) custom-call(bf16[256,1536]{1,0:T(8,128)(2,1)S(1)} %bitcast.61, f32[256,128]{1,0:T(8,128)S(1)} %pad_maximum_fusion.3.trig_ref, ...), custom_call_target="tpu_custom_call" | custom-call | tf_op jit(solution)/shard_map/gather_inputs/pallas_call | solution.py:386
  90.9 1.7 copy-done.1
  92.5 1.0 copy-done.2
  93.5 0.8 copy-done.3
  94.3 1.7 copy-done.4
  96.1 0.7 reshape.132.gain_ref
  96.7 0.7 reshape.133.gain_ref
  97.4 0.6 maximum_convert_fusion.bias_ref
  98.0 15.6 %attend_forward.1 = (bf16[1024,1536]{1,0:T(8,128)(2,1)}, bf16[1024,640]{1,0:T(8,128)(2,1)}, bf16[1024,384]{1,0:T(8,128)(2,1)}, f32[1024,128]{1,0:T(8,128)}, bf16[1024,1536]{1,0:T(8,128)(2,1)}) custom-call(bf16[1024,1536]{1,0:T(8,128)(2,1)} %bitcast.66, bf16[1536,1024]{1,0:T(8,128)(2,1)} %bitcast.62, bf16[384,1536]{1,0:T(8,128)(2,1)} %copy-done.2, ...), custom_call_target="tpu_custom_call" | custom-call | flops 4831838208 | bytes 18874368 | tf_op jit(solution)/shard_map/attend_forward/pallas_call | solution.py:491
  113.6 15.9 %all-gather.3.cloned.1.call-done = bf16[1,2048,1536]{2,1,0:T(8,128)(2,1)} async-done(((bf16[1,256,1536]{2,1,0:T(8,128)(2,1)}), bf16[1,2048,1536]{2,1,0:T(8,128)(2,1)}) %all-gather.3.cloned.1.call-update) | async-done | bytes 6291472 | tf_op jit(solution)/shard_map/all_gather | solution.py:1466
  129.5 175.5 %mlp_ring.1 = (bf16[2048,1536]{1,0:T(8,128)(2,1)}, f32[256,1536]{1,0:T(8,128)}, bf16[4,256,1536]{2,1,0:T(8,128)(2,1)}, f32[256,1536]{1,0:T(8,128)}, f32[1,1536]{1,0:T(1,128)}, /*index=5*/bf16[3,1120,1536]{2,1,0:T(8,128)(2,1)}) custom-call(bf16[256,1536]{1,0:T(8,128)(2,1)} %bitcast.59, bf16[1024,1536]{1,0:T(8,128)(2,1)} %get-tuple-element.36.part_ref, ...), custom_call_target="tpu_custom_call" | custom-call | tf_op jit(solution)/shard_map/mlp_ring/pallas_call | solution.py:888
  305.1 163.4 %attend_backward.1 = (f32[256,1536]{1,0:T(8,128)}, bf16[256,1536]{1,0:T(8,128)(2,1)}, f32[8,1536]{1,0:T(8,128)}, bf16[4,192,1024]{2,1,0:T(8,128)(2,1)}, bf16[3,1120,1536]{2,1,0:T(8,128)(2,1)}) custom-call(bf16[1024,1536]{1,0:T(8,128)(2,1)} %bitcast.68, bf16[1024,640]{1,0:T(8,128)(2,1)} %get-tuple-element.38.heads_ref, ...), custom_call_target="tpu_custom_call" | custom-call | tf_op jit(solution)/shard_map/attend_backward/pallas_call | solution.py:1352
  468.5 0.9 fusion.19
  469.4 0.7 slice.122
  470.1 1.8 convert_element_type.62
  471.9 0.1 slice_bitcast_fusion.3
  472.1 15.0 %add_bitcast_fusion = (f32[1120,1536]{1,0:T(8,128)}, f32[1120,1536]{1,0:T(8,128)}, f32[1120,1536]{1,0:T(8,128)}) fusion(bf16[3,1120,1536]{2,1,0:T(8,128)(2,1)} %get-tuple-element.51, bf16[3,1120,1536]{2,1,0:T(8,128)(2,1)} %get-tuple-element.46.units_ref), kind=kLoop, calls=%fused_computation | loop fusion | flops 15482880 | bytes 41287680 | tf_op jit(solution)/shard_map/add | solution.py:1536
  487.4 0.6 constant_dynamic-slice_fusion.1
  488.0 0.6 constant_dynamic-slice_fusion
  488.7 0.6 fusion.18
  489.3 1.2 pad_maximum_fusion
  490.5 0.9 copy.30
  491.3 1.1 copy.31
  (31 shorter events, 0.5 us)
Async XLA Ops:
  7.2 6.5 %copy-start = (bf16[1,256,1536]{2,1,0:T(8,128)(2,1)S(1)}, bf16[1,256,1536]{2,1,0:T(8,128)(2,1)}, u32[]{:S(2)}) copy-start(bf16[1,256,1536]{2,1,0:T(8,128)(2,1)} %param.11) | copy-start | bytes 2359300
  7.2 122.4 %all-gather.3.cloned.1.call-start = ((), (), s32[]{:S(2)}) async-start(), calls=%async_computation | async-start | bytes 7077888 | tf_op jit(solution)/shard_map/all_gather | solution.py:1466
  90.9 1.7 copy-start.1
  92.5 1.0 copy-start.2
  93.5 0.8 copy-start.3
  94.3 1.7 copy-start.4
  487.1 3.4 copy-start.6
  487.1 4.2 copy-start.5
  487.4 5.1 %copy-start.7 = (f32[192,2048]{1,0:T(8,128)}, f32[192,2048]{1,0:T(8,128)S(1)}, u32[]{:S(2)}) copy-start(f32[192,2048]{1,0:T(8,128)S(1)} %fusion.6) | copy-start | bytes 4718596
Sparse Core Ops, SparseCore 0:
  10.2 119.2 all-gather.2
